TPU v7x, 1024 devices: a whole 4x4x32 slice. The times are simulated.
1024 devices in a mesh: cuts: 16 (over z_lo), energy: 8 (over z_hi, y), group: 8 (over x, core).
Axes of the slice: x: 4, y: 4, z: 32 (z_hi: 2, z_lo: 16; z = z_hi * 16 + z_lo), core: 2. Of those that a mesh axis runs over, the one named last changes fastest.
Arguments:
- transfer: float32 [8, 48, 512, 512], P('energy', 'cuts'), may hold values from -1.5 to 1.5
- source: float32 [8, 24576, 1024], P('energy', 'cuts', 'group'), may hold values from -4 to 4
- coupling: bfloat16 [512, 512], replicated, may hold values from -0.25 to 0.25
- strength: float32 [8], replicated, may hold values from 0.2 to 1
- mode_shift: int32 [8], replicated, may hold values from 0 to 7, as said below
Outputs:
- green: float32 [8, 24576, 1024], P('energy', 'cuts', 'group')
- scattered: float32 [8, 24576, 1024], P('energy', 'cuts', 'group')
Inputs may be any that keep to these rules, and one draw needn't show every extreme that they name: `mode_shift`: every energy offset of 0 to 7 is taken by at least one mode.
All inputs are finite; a program needn't handle non-finite values.
Results may differ from a plain program's by a relative error of at most 0.0035.
Values sent between devices are 32-bit elements; how exact they have to be, the bound alone decides.
A program may use at most 64 MiB of HBM per device.

v0:
```python
import jax
import jax.numpy as jnp
from jax import lax
from jax.sharding import PartitionSpec as P


def shifted(value, axis, by):
    devices = lax.axis_size(axis)
    pairs = [(i, i + by) for i in range(devices) if 0 <= i + by < devices]
    return lax.ppermute(value, axis, pairs)


def copy_for_each(value, axis):
    copies = jnp.broadcast_to(value, (lax.axis_size(axis), *value.shape))
    return lax.all_to_all(copies, axis, split_axis=0, concat_axis=0, tiled=True)


def of_everyone(value, axis):
    return copy_for_each(value, axis).sum(axis=0)


def padded(value, sides, width):
    for axis, dim in sides:
        devices, length = (lax.axis_size(axis), value.shape[dim])
        up = [(i, (i + 1) % devices) for i in range(devices - 1)]
        down = [(j, i) for i, j in up]
        last = lax.slice_in_dim(value, length - width, length, axis=dim)
        initial = lax.slice_in_dim(value, 0, width, axis=dim)
        before = lax.ppermute(last, axis, up)
        after = lax.ppermute(initial, axis, down)
        value = jnp.concatenate([before, value, after], axis=dim)
    return value


def joined_along(tiles, dim):
    tiles = jnp.moveaxis(tiles, 0, dim)
    lengths = tiles.shape
    return tiles.reshape(*lengths[:dim], lengths[dim] * lengths[dim + 1], *lengths[dim + 2 :])


def collect(value, axis, dim):
    tiles = copy_for_each(value, axis)
    return joined_along(tiles, dim)


def matmul(left, right):
    return jnp.dot(left, right, precision=lax.Precision.HIGHEST, preferred_element_type=jnp.float32)


def body(transfer, source, coupling, strength, mode_shift):
    mats = transfer[0]
    count = mats.shape[0]
    orbs = mats.shape[1]
    srcs = source[0].reshape(count, orbs, source.shape[2])
    locals_list = []
    products = []
    for block in range(count):
        if block == 0:
            state = srcs[0]
            product = mats[0]
        else:
            state = matmul(mats[block], state) + srcs[block]
            product = matmul(mats[block], product)
        locals_list.append(state)
        products.append(product)
    composite = products[-1]
    offset = locals_list[-1]

    def advance(step, incoming):
        leaving = matmul(composite, incoming) + offset
        return shifted(leaving, "cuts", 1)

    incoming = lax.fori_loop(0, lax.axis_size("cuts") - 1, advance, jnp.zeros_like(offset))
    green = jnp.stack(
        [locals_list[block] + matmul(products[block], incoming) for block in range(count)]
    )
    partial_sq = jnp.sum(green * green, axis=2)
    totals = of_everyone(partial_sq, "group")
    density = totals / (green.shape[2] * lax.axis_size("group"))
    edges = padded(density, (("cuts", 0),), 1)
    smoothed = density + 0.5 * (edges[:-2] + edges[2:])
    every_energy = collect(smoothed[None], "energy", 0)
    points = every_energy.shape[0]
    here = lax.axis_index("energy")
    goal_value = (here + mode_shift) % points
    onehot = (goal_value[:, None] == jnp.arange(points, dtype=jnp.int32)[None, :]).astype(
        jnp.float32
    )
    weights = jnp.sum(strength[:, None] * onehot, axis=0)
    selfen = jnp.einsum("f,fko->ko", weights, every_energy, precision=lax.Precision.HIGHEST)
    low = green.astype(jnp.bfloat16)
    inner = jnp.einsum("oi,kon->kin", coupling, low, preferred_element_type=jnp.float32)
    scaled = (inner * selfen[:, :, None]).astype(jnp.bfloat16)
    scattered = jnp.einsum("io,kon->kin", coupling, scaled, preferred_element_type=jnp.float32)
    width = green.shape[2]
    return (green.reshape(1, count * orbs, width), scattered.reshape(1, count * orbs, width))


def solution(mesh):
    in_specs = (P("energy", "cuts", None, None), P("energy", "cuts", "group"), P(), P(), P())
    out_specs = (P("energy", "cuts", "group"), P("energy", "cuts", "group"))
    return jax.shard_map(body, mesh=mesh, in_specs=in_specs, out_specs=out_specs, check_vma=False)
```

profile of v0, /device:TPU:96, one launch (start us, length us, event | category | flops | bytes accessed | tf_op | source)
XLA Modules:
  0.0 266.6 jit_solution(81119311164005681)
XLA Ops:
  0.6 3.4 %fusion.11 = f32[512,512]{1,0:T(8,128)S(1)} fusion(f32[1,3,512,512]{3,2,1,0:T(8,128)} %param.7), kind=kOutput, calls=%fused_computation.19 | convolution fusion | flops 1610612736 | bytes 3145728 | tf_op jit(solution)/shard_map/dot_general | solution.py:47
  4.1 5.7 %fusion.8 = f32[512,512]{1,0:T(8,128)} fusion(f32[512,512]{1,0:T(8,128)S(1)} %fusion.11, f32[1,3,512,512]{3,2,1,0:T(8,128)} %param.7), kind=kOutput, calls=%fused_computation.16 | convolution fusion | flops 1610612736 | bytes 3145728 | tf_op jit(solution)/shard_map/dot_general | solution.py:47
  9.8 1.6 copy.32
  11.3 2.3 convolution_add_fusion.3
  13.7 2.3 fusion.2
  16.1 170.7 %while.10 = (s32[]{:T(128)}, f32[512,128]{1,0:T(8,128)S(1)}, f32[512,512]{1,0:T(8,128)S(1)}, f32[512,128]{1,0:T(8,128)S(1)}, s32[]{:T(128)}) while((s32[]{:T(128)}, f32[512,128]{1,0:T(8,128)S(1)}, f32[512,512]{1,0:T(8,128)S(1)}, f32[512,128]{1,0:T(8,128)S(1)}, s32[]{:T(128)}) %tuple.30), condition=%wide.region_1.0_spmd, body=%wide.region_0.0_spmd.sunk | while | flops 402718720 | bytes 2883685 | solution.py:73
  17.2 5.0 %collective-permute-start = (f32[512,128]{1,0:T(8,128)S(1)}, f32[512,128]{1,0:T(8,128)S(1)}, u32[]{:S(2)}, u32[]{:S(2)}) collective-permute-start(f32[512,128]{1,0:T(8,128)S(1)} %convolution_add_fusion.5), channel_id=1, source_target_pairs={{0,64},{64,128},{128,192},{192,256},{256,320},{320,384},{384,448},... | collective-permute-start | bytes 786440 | tf_op jit(solution)/shard_map/while/body/eval_jaxpr/ppermute | solution.py:10
  22.3 5.5 %collective-permute-done = f32[512,128]{1,0:T(8,128)S(1)} collective-permute-done((f32[512,128]{1,0:T(8,128)S(1)}, f32[512,128]{1,0:T(8,128)S(1)}, u32[]{:S(2)}, u32[]{:S(2)}) %collective-permute-start) | collective-permute-done | bytes 262176 | tf_op jit(solution)/shard_map/while/body/eval_jaxpr/ppermute | solution.py:10
  28.8 5.6 %collective-permute-start = (f32[512,128]{1,0:T(8,128)S(1)}, f32[512,128]{1,0:T(8,128)S(1)}, u32[]{:S(2)}, u32[]{:S(2)}) collective-permute-start(f32[512,128]{1,0:T(8,128)S(1)} %convolution_add_fusion.5), channel_id=1, source_target_pairs={{0,64},{64,128},{128,192},{192,256},{256,320},{320,384},{384,448},... | collective-permute-start | bytes 786440 | tf_op jit(solution)/shard_map/while/body/eval_jaxpr/ppermute | solution.py:10
  34.4 4.7 %collective-permute-done = f32[512,128]{1,0:T(8,128)S(1)} collective-permute-done((f32[512,128]{1,0:T(8,128)S(1)}, f32[512,128]{1,0:T(8,128)S(1)}, u32[]{:S(2)}, u32[]{:S(2)}) %collective-permute-start) | collective-permute-done | bytes 262176 | tf_op jit(solution)/shard_map/while/body/eval_jaxpr/ppermute | solution.py:10
  40.1 5.6 %collective-permute-start = (f32[512,128]{1,0:T(8,128)S(1)}, f32[512,128]{1,0:T(8,128)S(1)}, u32[]{:S(2)}, u32[]{:S(2)}) collective-permute-start(f32[512,128]{1,0:T(8,128)S(1)} %convolution_add_fusion.5), channel_id=1, source_target_pairs={{0,64},{64,128},{128,192},{192,256},{256,320},{320,384},{384,448},... | collective-permute-start | bytes 786440 | tf_op jit(solution)/shard_map/while/body/eval_jaxpr/ppermute | solution.py:10
  45.7 9.8 %collective-permute-done = f32[512,128]{1,0:T(8,128)S(1)} collective-permute-done((f32[512,128]{1,0:T(8,128)S(1)}, f32[512,128]{1,0:T(8,128)S(1)}, u32[]{:S(2)}, u32[]{:S(2)}) %collective-permute-start) | collective-permute-done | bytes 262176 | tf_op jit(solution)/shard_map/while/body/eval_jaxpr/ppermute | solution.py:10
  56.5 1.9 collective-permute-start
  58.4 9.2 %collective-permute-done = f32[512,128]{1,0:T(8,128)S(1)} collective-permute-done((f32[512,128]{1,0:T(8,128)S(1)}, f32[512,128]{1,0:T(8,128)S(1)}, u32[]{:S(2)}, u32[]{:S(2)}) %collective-permute-start) | collective-permute-done | bytes 262176 | tf_op jit(solution)/shard_map/while/body/eval_jaxpr/ppermute | solution.py:10
  68.6 1.9 collective-permute-start
  70.5 8.3 %collective-permute-done = f32[512,128]{1,0:T(8,128)S(1)} collective-permute-done((f32[512,128]{1,0:T(8,128)S(1)}, f32[512,128]{1,0:T(8,128)S(1)}, u32[]{:S(2)}, u32[]{:S(2)}) %collective-permute-start) | collective-permute-done | bytes 262176 | tf_op jit(solution)/shard_map/while/body/eval_jaxpr/ppermute | solution.py:10
  78.8 1.0 convolution_add_fusion.5
  79.8 3.7 %collective-permute-start = (f32[512,128]{1,0:T(8,128)S(1)}, f32[512,128]{1,0:T(8,128)S(1)}, u32[]{:S(2)}, u32[]{:S(2)}) collective-permute-start(f32[512,128]{1,0:T(8,128)S(1)} %convolution_add_fusion.5), channel_id=1, source_target_pairs={{0,64},{64,128},{128,192},{192,256},{256,320},{320,384},{384,448},... | collective-permute-start | bytes 786440 | tf_op jit(solution)/shard_map/while/body/eval_jaxpr/ppermute | solution.py:10
  83.5 5.8 %collective-permute-done = f32[512,128]{1,0:T(8,128)S(1)} collective-permute-done((f32[512,128]{1,0:T(8,128)S(1)}, f32[512,128]{1,0:T(8,128)S(1)}, u32[]{:S(2)}, u32[]{:S(2)}) %collective-permute-start) | collective-permute-done | bytes 262176 | tf_op jit(solution)/shard_map/while/body/eval_jaxpr/ppermute | solution.py:10
  90.3 5.6 %collective-permute-start = (f32[512,128]{1,0:T(8,128)S(1)}, f32[512,128]{1,0:T(8,128)S(1)}, u32[]{:S(2)}, u32[]{:S(2)}) collective-permute-start(f32[512,128]{1,0:T(8,128)S(1)} %convolution_add_fusion.5), channel_id=1, source_target_pairs={{0,64},{64,128},{128,192},{192,256},{256,320},{320,384},{384,448},... | collective-permute-start | bytes 786440 | tf_op jit(solution)/shard_map/while/body/eval_jaxpr/ppermute | solution.py:10
  95.9 5.0 %collective-permute-done = f32[512,128]{1,0:T(8,128)S(1)} collective-permute-done((f32[512,128]{1,0:T(8,128)S(1)}, f32[512,128]{1,0:T(8,128)S(1)}, u32[]{:S(2)}, u32[]{:S(2)}) %collective-permute-start) | collective-permute-done | bytes 262176 | tf_op jit(solution)/shard_map/while/body/eval_jaxpr/ppermute | solution.py:10
  101.9 5.6 %collective-permute-start = (f32[512,128]{1,0:T(8,128)S(1)}, f32[512,128]{1,0:T(8,128)S(1)}, u32[]{:S(2)}, u32[]{:S(2)}) collective-permute-start(f32[512,128]{1,0:T(8,128)S(1)} %convolution_add_fusion.5), channel_id=1, source_target_pairs={{0,64},{64,128},{128,192},{192,256},{256,320},{320,384},{384,448},... | collective-permute-start | bytes 786440 | tf_op jit(solution)/shard_map/while/body/eval_jaxpr/ppermute | solution.py:10
  107.5 4.1 %collective-permute-done = f32[512,128]{1,0:T(8,128)S(1)} collective-permute-done((f32[512,128]{1,0:T(8,128)S(1)}, f32[512,128]{1,0:T(8,128)S(1)}, u32[]{:S(2)}, u32[]{:S(2)}) %collective-permute-start) | collective-permute-done | bytes 262176 | tf_op jit(solution)/shard_map/while/body/eval_jaxpr/ppermute | solution.py:10
  112.6 5.6 %collective-permute-start = (f32[512,128]{1,0:T(8,128)S(1)}, f32[512,128]{1,0:T(8,128)S(1)}, u32[]{:S(2)}, u32[]{:S(2)}) collective-permute-start(f32[512,128]{1,0:T(8,128)S(1)} %convolution_add_fusion.5), channel_id=1, source_target_pairs={{0,64},{64,128},{128,192},{192,256},{256,320},{320,384},{384,448},... | collective-permute-start | bytes 786440 | tf_op jit(solution)/shard_map/while/body/eval_jaxpr/ppermute | solution.py:10
  118.2 3.9 %collective-permute-done = f32[512,128]{1,0:T(8,128)S(1)} collective-permute-done((f32[512,128]{1,0:T(8,128)S(1)}, f32[512,128]{1,0:T(8,128)S(1)}, u32[]{:S(2)}, u32[]{:S(2)}) %collective-permute-start) | collective-permute-done | bytes 262176 | tf_op jit(solution)/shard_map/while/body/eval_jaxpr/ppermute | solution.py:10
  123.1 5.6 %collective-permute-start = (f32[512,128]{1,0:T(8,128)S(1)}, f32[512,128]{1,0:T(8,128)S(1)}, u32[]{:S(2)}, u32[]{:S(2)}) collective-permute-start(f32[512,128]{1,0:T(8,128)S(1)} %convolution_add_fusion.5), channel_id=1, source_target_pairs={{0,64},{64,128},{128,192},{192,256},{256,320},{320,384},{384,448},... | collective-permute-start | bytes 786440 | tf_op jit(solution)/shard_map/while/body/eval_jaxpr/ppermute | solution.py:10
  128.7 3.9 %collective-permute-done = f32[512,128]{1,0:T(8,128)S(1)} collective-permute-done((f32[512,128]{1,0:T(8,128)S(1)}, f32[512,128]{1,0:T(8,128)S(1)}, u32[]{:S(2)}, u32[]{:S(2)}) %collective-permute-start) | collective-permute-done | bytes 262176 | tf_op jit(solution)/shard_map/while/body/eval_jaxpr/ppermute | solution.py:10
  133.5 5.6 %collective-permute-start = (f32[512,128]{1,0:T(8,128)S(1)}, f32[512,128]{1,0:T(8,128)S(1)}, u32[]{:S(2)}, u32[]{:S(2)}) collective-permute-start(f32[512,128]{1,0:T(8,128)S(1)} %convolution_add_fusion.5), channel_id=1, source_target_pairs={{0,64},{64,128},{128,192},{192,256},{256,320},{320,384},{384,448},... | collective-permute-start | bytes 786440 | tf_op jit(solution)/shard_map/while/body/eval_jaxpr/ppermute | solution.py:10
  139.1 3.9 %collective-permute-done = f32[512,128]{1,0:T(8,128)S(1)} collective-permute-done((f32[512,128]{1,0:T(8,128)S(1)}, f32[512,128]{1,0:T(8,128)S(1)}, u32[]{:S(2)}, u32[]{:S(2)}) %collective-permute-start) | collective-permute-done | bytes 262176 | tf_op jit(solution)/shard_map/while/body/eval_jaxpr/ppermute | solution.py:10
  144.0 5.6 %collective-permute-start = (f32[512,128]{1,0:T(8,128)S(1)}, f32[512,128]{1,0:T(8,128)S(1)}, u32[]{:S(2)}, u32[]{:S(2)}) collective-permute-start(f32[512,128]{1,0:T(8,128)S(1)} %convolution_add_fusion.5), channel_id=1, source_target_pairs={{0,64},{64,128},{128,192},{192,256},{256,320},{320,384},{384,448},... | collective-permute-start | bytes 786440 | tf_op jit(solution)/shard_map/while/body/eval_jaxpr/ppermute | solution.py:10
  149.6 4.2 %collective-permute-done = f32[512,128]{1,0:T(8,128)S(1)} collective-permute-done((f32[512,128]{1,0:T(8,128)S(1)}, f32[512,128]{1,0:T(8,128)S(1)}, u32[]{:S(2)}, u32[]{:S(2)}) %collective-permute-start) | collective-permute-done | bytes 262176 | tf_op jit(solution)/shard_map/while/body/eval_jaxpr/ppermute | solution.py:10
  154.8 5.6 %collective-permute-start = (f32[512,128]{1,0:T(8,128)S(1)}, f32[512,128]{1,0:T(8,128)S(1)}, u32[]{:S(2)}, u32[]{:S(2)}) collective-permute-start(f32[512,128]{1,0:T(8,128)S(1)} %convolution_add_fusion.5), channel_id=1, source_target_pairs={{0,64},{64,128},{128,192},{192,256},{256,320},{320,384},{384,448},... | collective-permute-start | bytes 786440 | tf_op jit(solution)/shard_map/while/body/eval_jaxpr/ppermute | solution.py:10
  160.4 5.4 %collective-permute-done = f32[512,128]{1,0:T(8,128)S(1)} collective-permute-done((f32[512,128]{1,0:T(8,128)S(1)}, f32[512,128]{1,0:T(8,128)S(1)}, u32[]{:S(2)}, u32[]{:S(2)}) %collective-permute-start) | collective-permute-done | bytes 262176 | tf_op jit(solution)/shard_map/while/body/eval_jaxpr/ppermute | solution.py:10
  166.8 5.6 %collective-permute-start = (f32[512,128]{1,0:T(8,128)S(1)}, f32[512,128]{1,0:T(8,128)S(1)}, u32[]{:S(2)}, u32[]{:S(2)}) collective-permute-start(f32[512,128]{1,0:T(8,128)S(1)} %convolution_add_fusion.5), channel_id=1, source_target_pairs={{0,64},{64,128},{128,192},{192,256},{256,320},{320,384},{384,448},... | collective-permute-start | bytes 786440 | tf_op jit(solution)/shard_map/while/body/eval_jaxpr/ppermute | solution.py:10
  172.4 3.9 %collective-permute-done = f32[512,128]{1,0:T(8,128)S(1)} collective-permute-done((f32[512,128]{1,0:T(8,128)S(1)}, f32[512,128]{1,0:T(8,128)S(1)}, u32[]{:S(2)}, u32[]{:S(2)}) %collective-permute-start) | collective-permute-done | bytes 262176 | tf_op jit(solution)/shard_map/while/body/eval_jaxpr/ppermute | solution.py:10
  177.2 5.6 %collective-permute-start = (f32[512,128]{1,0:T(8,128)S(1)}, f32[512,128]{1,0:T(8,128)S(1)}, u32[]{:S(2)}, u32[]{:S(2)}) collective-permute-start(f32[512,128]{1,0:T(8,128)S(1)} %convolution_add_fusion.5), channel_id=1, source_target_pairs={{0,64},{64,128},{128,192},{192,256},{256,320},{320,384},{384,448},... | collective-permute-start | bytes 786440 | tf_op jit(solution)/shard_map/while/body/eval_jaxpr/ppermute | solution.py:10
  182.9 3.9 %collective-permute-done = f32[512,128]{1,0:T(8,128)S(1)} collective-permute-done((f32[512,128]{1,0:T(8,128)S(1)}, f32[512,128]{1,0:T(8,128)S(1)}, u32[]{:S(2)}, u32[]{:S(2)}) %collective-permute-start) | collective-permute-done | bytes 262176 | tf_op jit(solution)/shard_map/while/body/eval_jaxpr/ppermute | solution.py:10
  186.7 3.0 %fusion.5 = f32[1,512,128]{2,1,0:T(8,128)S(1)} fusion(f32[512,128]{1,0:T(8,128)S(1)} %get-tuple-element.102, f32[512,512]{1,0:T(8,128)} %fusion.8, f32[512,128]{1,0:T(8,128)S(1)} %get-tuple-element.24), kind=kOutput, calls=%fused_computation.11 | convolution fusion | flops 402718720 | bytes 1835008 | tf_op jit(solution)/shard_map/dot_general | solution.py:47
  189.8 1.9 fusion.6
  191.7 2.3 fusion.4
  194.0 1.0 multiply_reduce_fusion
  195.0 8.0 %all_to_all.10 = f32[8,3,512]{2,1,0:T(4,128)S(1)} all-to-all(f32[8,3,512]{2,1,0:T(4,128)S(1)} %broadcast_in_dim.7), channel_id=1, replica_groups=mesh['cuts'=16,'energy'=8,'group'=8] {'group'}, dimensions={0} | all-to-all | bytes 98304 | tf_op jit(solution)/shard_map/all_to_all | solution.py:15
  203.1 5.6 %collective-permute-start.1 = (f32[1,512]{1,0:T(1,128)S(1)}, f32[1,512]{1,0:T(1,128)S(1)}, u32[]{:S(2)}, u32[]{:S(2)}) collective-permute-start(f32[1,512]{1,0:T(1,128)S(1)} %get-tuple-element.59), channel_id=1, source_target_pairs={{0,64},{64,128},{128,192},{192,256},{256,320},{320,384},{384,448},... | collective-permute-start | bytes 6152 | tf_op jit(solution)/shard_map/ppermute | solution.py:29
  208.7 1.9 collective-permute-start.2
  210.6 4.8 %collective-permute-done.2 = f32[1,512]{1,0:T(1,128)S(1)} collective-permute-done((f32[1,512]{1,0:T(1,128)S(1)}, f32[1,512]{1,0:T(1,128)S(1)}, u32[]{:S(2)}, u32[]{:S(2)}) %collective-permute-start.2) | collective-permute-done | bytes 2080 | tf_op jit(solution)/shard_map/ppermute | solution.py:30
  216.0 24.0 %all-to-all-start.1 = ((f32[8,1,3,512]{3,1,2,0:T(1,128)}), f32[8,1,3,512]{3,1,2,0:T(1,128)S(1)}, u32[]{:S(2)}, u32[]{:S(2)}) async-start(f32[8,1,3,512]{3,1,2,0:T(1,128)} %broadcast_in_dim.16), calls=%async_computation.1 | async-start | bytes 98304 | tf_op jit(solution)/shard_map/all_to_all | solution.py:15
  240.1 24.5 %all-to-all-done.1 = f32[8,1,3,512]{3,1,2,0:T(1,128)S(1)} async-done(((f32[8,1,3,512]{3,1,2,0:T(1,128)}), f32[8,1,3,512]{3,1,2,0:T(1,128)S(1)}, u32[]{:S(2)}, u32[]{:S(2)}) %all-to-all-start.1) | async-done | bytes 49184 | tf_op jit(solution)/shard_map/all_to_all | solution.py:15
  265.5 1.2 copy.37
  (35 shorter events, 15.5 us)
Async XLA Ops:
  0.6 264.2 %copy-start = (bf16[512,512]{1,0:T(8,128)(2,1)S(1)}, bf16[512,512]{1,0:T(8,128)(2,1)}, u32[]{:S(2)}) copy-start(bf16[512,512]{1,0:T(8,128)(2,1)} %param.9) | copy-start | bytes 1572868
  13.7 2.4 copy-start.1
  17.2 10.6 %collective-permute-start = (f32[512,128]{1,0:T(8,128)S(1)}, f32[512,128]{1,0:T(8,128)S(1)}, u32[]{:S(2)}, u32[]{:S(2)}) collective-permute-start(f32[512,128]{1,0:T(8,128)S(1)} %convolution_add_fusion.5), channel_id=1, source_target_pairs={{0,64},{64,128},{128,192},{192,256},{256,320},{320,384},{384,448},... | collective-permute-start | bytes 786440 | tf_op jit(solution)/shard_map/while/body/eval_jaxpr/ppermute | solution.py:10
  28.8 10.3 %collective-permute-start = (f32[512,128]{1,0:T(8,128)S(1)}, f32[512,128]{1,0:T(8,128)S(1)}, u32[]{:S(2)}, u32[]{:S(2)}) collective-permute-start(f32[512,128]{1,0:T(8,128)S(1)} %convolution_add_fusion.5), channel_id=1, source_target_pairs={{0,64},{64,128},{128,192},{192,256},{256,320},{320,384},{384,448},... | collective-permute-start | bytes 786440 | tf_op jit(solution)/shard_map/while/body/eval_jaxpr/ppermute | solution.py:10
  40.1 15.4 %collective-permute-start = (f32[512,128]{1,0:T(8,128)S(1)}, f32[512,128]{1,0:T(8,128)S(1)}, u32[]{:S(2)}, u32[]{:S(2)}) collective-permute-start(f32[512,128]{1,0:T(8,128)S(1)} %convolution_add_fusion.5), channel_id=1, source_target_pairs={{0,64},{64,128},{128,192},{192,256},{256,320},{320,384},{384,448},... | collective-permute-start | bytes 786440 | tf_op jit(solution)/shard_map/while/body/eval_jaxpr/ppermute | solution.py:10
  56.5 11.1 %collective-permute-start = (f32[512,128]{1,0:T(8,128)S(1)}, f32[512,128]{1,0:T(8,128)S(1)}, u32[]{:S(2)}, u32[]{:S(2)}) collective-permute-start(f32[512,128]{1,0:T(8,128)S(1)} %convolution_add_fusion.5), channel_id=1, source_target_pairs={{0,64},{64,128},{128,192},{192,256},{256,320},{320,384},{384,448},... | collective-permute-start | bytes 786440 | tf_op jit(solution)/shard_map/while/body/eval_jaxpr/ppermute | solution.py:10
  68.6 10.2 %collective-permute-start = (f32[512,128]{1,0:T(8,128)S(1)}, f32[512,128]{1,0:T(8,128)S(1)}, u32[]{:S(2)}, u32[]{:S(2)}) collective-permute-start(f32[512,128]{1,0:T(8,128)S(1)} %convolution_add_fusion.5), channel_id=1, source_target_pairs={{0,64},{64,128},{128,192},{192,256},{256,320},{320,384},{384,448},... | collective-permute-start | bytes 786440 | tf_op jit(solution)/shard_map/while/body/eval_jaxpr/ppermute | solution.py:10
  79.8 9.5 %collective-permute-start = (f32[512,128]{1,0:T(8,128)S(1)}, f32[512,128]{1,0:T(8,128)S(1)}, u32[]{:S(2)}, u32[]{:S(2)}) collective-permute-start(f32[512,128]{1,0:T(8,128)S(1)} %convolution_add_fusion.5), channel_id=1, source_target_pairs={{0,64},{64,128},{128,192},{192,256},{256,320},{320,384},{384,448},... | collective-permute-start | bytes 786440 | tf_op jit(solution)/shard_map/while/body/eval_jaxpr/ppermute | solution.py:10
  90.3 10.6 %collective-permute-start = (f32[512,128]{1,0:T(8,128)S(1)}, f32[512,128]{1,0:T(8,128)S(1)}, u32[]{:S(2)}, u32[]{:S(2)}) collective-permute-start(f32[512,128]{1,0:T(8,128)S(1)} %convolution_add_fusion.5), channel_id=1, source_target_pairs={{0,64},{64,128},{128,192},{192,256},{256,320},{320,384},{384,448},... | collective-permute-start | bytes 786440 | tf_op jit(solution)/shard_map/while/body/eval_jaxpr/ppermute | solution.py:10
  101.9 9.7 %collective-permute-start = (f32[512,128]{1,0:T(8,128)S(1)}, f32[512,128]{1,0:T(8,128)S(1)}, u32[]{:S(2)}, u32[]{:S(2)}) collective-permute-start(f32[512,128]{1,0:T(8,128)S(1)} %convolution_add_fusion.5), channel_id=1, source_target_pairs={{0,64},{64,128},{128,192},{192,256},{256,320},{320,384},{384,448},... | collective-permute-start | bytes 786440 | tf_op jit(solution)/shard_map/while/body/eval_jaxpr/ppermute | solution.py:10
  112.6 9.5 %collective-permute-start = (f32[512,128]{1,0:T(8,128)S(1)}, f32[512,128]{1,0:T(8,128)S(1)}, u32[]{:S(2)}, u32[]{:S(2)}) collective-permute-start(f32[512,128]{1,0:T(8,128)S(1)} %convolution_add_fusion.5), channel_id=1, source_target_pairs={{0,64},{64,128},{128,192},{192,256},{256,320},{320,384},{384,448},... | collective-permute-start | bytes 786440 | tf_op jit(solution)/shard_map/while/body/eval_jaxpr/ppermute | solution.py:10
  123.1 9.5 %collective-permute-start = (f32[512,128]{1,0:T(8,128)S(1)}, f32[512,128]{1,0:T(8,128)S(1)}, u32[]{:S(2)}, u32[]{:S(2)}) collective-permute-start(f32[512,128]{1,0:T(8,128)S(1)} %convolution_add_fusion.5), channel_id=1, source_target_pairs={{0,64},{64,128},{128,192},{192,256},{256,320},{320,384},{384,448},... | collective-permute-start | bytes 786440 | tf_op jit(solution)/shard_map/while/body/eval_jaxpr/ppermute | solution.py:10
  133.5 9.5 %collective-permute-start = (f32[512,128]{1,0:T(8,128)S(1)}, f32[512,128]{1,0:T(8,128)S(1)}, u32[]{:S(2)}, u32[]{:S(2)}) collective-permute-start(f32[512,128]{1,0:T(8,128)S(1)} %convolution_add_fusion.5), channel_id=1, source_target_pairs={{0,64},{64,128},{128,192},{192,256},{256,320},{320,384},{384,448},... | collective-permute-start | bytes 786440 | tf_op jit(solution)/shard_map/while/body/eval_jaxpr/ppermute | solution.py:10
  144.0 9.8 %collective-permute-start = (f32[512,128]{1,0:T(8,128)S(1)}, f32[512,128]{1,0:T(8,128)S(1)}, u32[]{:S(2)}, u32[]{:S(2)}) collective-permute-start(f32[512,128]{1,0:T(8,128)S(1)} %convolution_add_fusion.5), channel_id=1, source_target_pairs={{0,64},{64,128},{128,192},{192,256},{256,320},{320,384},{384,448},... | collective-permute-start | bytes 786440 | tf_op jit(solution)/shard_map/while/body/eval_jaxpr/ppermute | solution.py:10
  154.8 11.0 %collective-permute-start = (f32[512,128]{1,0:T(8,128)S(1)}, f32[512,128]{1,0:T(8,128)S(1)}, u32[]{:S(2)}, u32[]{:S(2)}) collective-permute-start(f32[512,128]{1,0:T(8,128)S(1)} %convolution_add_fusion.5), channel_id=1, source_target_pairs={{0,64},{64,128},{128,192},{192,256},{256,320},{320,384},{384,448},... | collective-permute-start | bytes 786440 | tf_op jit(solution)/shard_map/while/body/eval_jaxpr/ppermute | solution.py:10
  166.8 9.5 %collective-permute-start = (f32[512,128]{1,0:T(8,128)S(1)}, f32[512,128]{1,0:T(8,128)S(1)}, u32[]{:S(2)}, u32[]{:S(2)}) collective-permute-start(f32[512,128]{1,0:T(8,128)S(1)} %convolution_add_fusion.5), channel_id=1, source_target_pairs={{0,64},{64,128},{128,192},{192,256},{256,320},{320,384},{384,448},... | collective-permute-start | bytes 786440 | tf_op jit(solution)/shard_map/while/body/eval_jaxpr/ppermute | solution.py:10
  177.2 9.5 %collective-permute-start = (f32[512,128]{1,0:T(8,128)S(1)}, f32[512,128]{1,0:T(8,128)S(1)}, u32[]{:S(2)}, u32[]{:S(2)}) collective-permute-start(f32[512,128]{1,0:T(8,128)S(1)} %convolution_add_fusion.5), channel_id=1, source_target_pairs={{0,64},{64,128},{128,192},{192,256},{256,320},{320,384},{384,448},... | collective-permute-start | bytes 786440 | tf_op jit(solution)/shard_map/while/body/eval_jaxpr/ppermute | solution.py:10
  189.8 50.2 %copy-start.2 = (s32[8]{0:T(128)S(1)}, s32[8]{0:T(128)}, u32[]{:S(2)}) copy-start(s32[8]{0:T(128)} %param.11) | copy-start | bytes 100
  189.8 50.2 %copy-start.3 = (f32[8]{0:T(128)S(1)}, f32[8]{0:T(128)}, u32[]{:S(2)}) copy-start(f32[8]{0:T(128)} %param.10) | copy-start | bytes 100
  203.1 7.5 %collective-permute-start.1 = (f32[1,512]{1,0:T(1,128)S(1)}, f32[1,512]{1,0:T(1,128)S(1)}, u32[]{:S(2)}, u32[]{:S(2)}) collective-permute-start(f32[1,512]{1,0:T(1,128)S(1)} %get-tuple-element.59), channel_id=1, source_target_pairs={{0,64},{64,128},{128,192},{192,256},{256,320},{320,384},{384,448},... | collective-permute-start | bytes 6152 | tf_op jit(solution)/shard_map/ppermute | solution.py:29
  208.7 6.7 %collective-permute-start.2 = (f32[1,512]{1,0:T(1,128)S(1)}, f32[1,512]{1,0:T(1,128)S(1)}, u32[]{:S(2)}, u32[]{:S(2)}) collective-permute-start(f32[1,512]{1,0:T(1,128)S(1)} %get-tuple-element.60), channel_id=1, source_target_pairs={{64,0},{128,64},{192,128},{256,192},{320,256},{384,320},{448,384},... | collective-permute-start | bytes 6152 | tf_op jit(solution)/shard_map/ppermute | solution.py:30
  216.0 48.6 %all-to-all-start.1 = ((f32[8,1,3,512]{3,1,2,0:T(1,128)}), f32[8,1,3,512]{3,1,2,0:T(1,128)S(1)}, u32[]{:S(2)}, u32[]{:S(2)}) async-start(f32[8,1,3,512]{3,1,2,0:T(1,128)} %broadcast_in_dim.16), calls=%async_computation.1 | async-start | bytes 98304 | tf_op jit(solution)/shard_map/all_to_all | solution.py:15
where the time goes:
time: 268 us; the launch traced here: 267 us
  waiting for transfers between devices  111 us (41%)
  starting transfers between devices  106 us (40%)
  matrix products  36.6 us (14%)
  blocking collectives  8 us (3%)
  local copies, waits for them, and re-layouts  3.42 us (1%)
    ppermute x15, waiting for transfers between devices, shifted(): return lax.ppermute(value, axis, pairs)  81.3 us
    ppermute x15, starting transfers between devices, shifted(): return lax.ppermute(value, axis, pairs)  74.2 us
    dot_general x22, matrix products, matmul(): jnp.dot(left, right, precision=lax.Precision.HIGHEST, preferred_element_t...  35.8 us
    all_to_all x1, waiting for transfers between devices, copy_for_each(): return lax.all_to_all(copies, axis, split_axis=0, concat_axis=0, tiled=True)  24.5 us
    all_to_all x1, starting transfers between devices, copy_for_each(): return lax.all_to_all(copies, axis, split_axis=0, concat_axis=0, tiled=True)  24 us
    all_to_all x1, blocking collectives, copy_for_each(): return lax.all_to_all(copies, axis, split_axis=0, concat_axis=0, tiled=True)  8 us
    ppermute x1, starting transfers between devices, padded(): before = lax.ppermute(last, axis, up)  5.6 us
  transfers between devices with their start and end apart: 18, of which 17 were waited for; matrix products, arithmetic and copies ran while one was open for 0% of the time, Pallas kernels for 0%

commit v1 on v0

v1 whole, which is shorter than its diff:
```python
import functools

import jax
import jax.numpy as jnp
from jax import lax
from jax.experimental import pallas as pl
from jax.experimental.pallas import tpu as pltpu
from jax.sharding import PartitionSpec as P

MESH = pl.DeviceIdType.MESH
F32, BF16 = jnp.float32, jnp.bfloat16
PIECES = 8
HALVES = 2


def halves(value):
    high = value.astype(BF16)
    return high, (value - high.astype(F32)).astype(BF16)


def nn(left, right):
    return jnp.dot(left, right, preferred_element_type=F32)


def nt(left, right):
    return lax.dot_general(left, right, (((1,), (1,)), ((), ())), preferred_element_type=F32)


def kernel(sizes, t_hbm, s_hbm, coup, w, green, scat, tb, sb, ah, al, bh, bl, t0h, t0l, p1h, p1l, ch, cl, p1, lt, xt, gt, inner,
           gout, sout, part, ga, ed, er, smb, ys, zs, zr, load, store, xs_sem, xr_sem, as_sem, ar_sem, es_sem, er_sem, ys_sem,
           yr_sem, z_sem, up_sem, dn_sem):
    cuts, energies, groups, count = sizes
    ny = energies // HALVES
    nz = HALVES * cuts
    j, e, q = lax.axis_index("cuts"), lax.axis_index("energy"), lax.axis_index("group")
    y = lax.rem(e, ny)
    z = (e // ny) * cuts + j
    orbs, cols = tb.shape[1], xt.shape[0]
    lanes = part.shape[1]
    strips = orbs // lanes
    width = cols // PIECES

    def along_z(step):
        there = lax.rem(z + step + nz, nz)
        return (lax.rem(there, cuts), (there // cuts) * ny + y, q)

    def along_group(step):
        return (j, e, lax.rem(q + step, groups))

    def along_y(step):
        return (j, (e // ny) * ny + lax.rem(y + step, ny), q)

    def local(src, dst, sem):
        return pltpu.make_async_copy(src, dst, sem)

    def remote(src, dst, send, recv, device):
        return pltpu.make_async_remote_copy(src_ref=src, dst_ref=dst, send_sem=send, recv_sem=recv, device_id=device, device_id_type=MESH)

    loads = [local(t_hbm.at[0, k], tb.at[k], load.at[k]) for k in range(count)]
    loads.append(local(s_hbm.at[0], sb, load.at[count]))
    for k in (0, 1, 3, 2):
        loads[k].start()

    barrier = pltpu.get_barrier_semaphore()
    near = [along_z(1), along_z(-1)] + [along_group(r) for r in range(1, groups)] + [along_y(r) for r in range(1, ny)]
    for device in near:
        pl.semaphore_signal(barrier, inc=1, device_id=device, device_id_type=MESH)
    pl.semaphore_wait(barrier, len(near))

    def greet(rnd):
        pl.semaphore_signal(up_sem.at[rnd], inc=1, device_id=along_z(2**rnd), device_id_type=MESH)
        pl.semaphore_signal(dn_sem.at[rnd], inc=1, device_id=along_z(-(2**rnd)), device_id_type=MESH)

    def met(rnd):
        pl.semaphore_wait(up_sem.at[rnd], 1)
        pl.semaphore_wait(dn_sem.at[rnd], 1)

    greet(0)

    loads[0].wait()
    high, low = halves(tb[0].T)
    t0h[...] = high
    t0l[...] = low
    loads[1].wait()
    high, low = halves(tb[1])
    ah[...] = high
    al[...] = low
    met(0)
    greet(1)
    p1[...] = nt(t0h[...], ah[...]) + (nt(t0l[...], ah[...]) + nt(t0h[...], al[...]))
    high, low = halves(p1[...])
    p1h[...] = high
    p1l[...] = low
    loads[3].wait()
    for k in range(count):
        lt[k] = sb[pl.ds(k * orbs, orbs), :].T
    met(1)
    greet(2)
    high, low = halves(lt[0])
    lt[1] = lt[1] + (nt(high, ah[...]) + (nt(low, ah[...]) + nt(high, al[...])))
    loads[2].wait()
    high, low = halves(tb[2])
    bh[...] = high
    bl[...] = low
    high, low = halves(lt[1])
    lt[2] = lt[2] + (nt(high, bh[...]) + (nt(low, bh[...]) + nt(high, bl[...])))

    def piece(p):
        rows = pl.ds(pl.multiple_of(p * width, width), width)
        return rows, remote(gt.at[2, rows], xt.at[rows], xs_sem.at[p], xr_sem.at[p], along_z(1))

    @pl.when(j == 0)
    def _():
        for k in range(count):
            gt[k] = lt[k]

        def send(p, _):
            piece(p)[1].start()
            return 0

        lax.fori_loop(0, PIECES, send, 0)

    p1[...] = nt(p1h[...], bh[...]) + (nt(p1l[...], bh[...]) + nt(p1h[...], bl[...]))
    high, low = halves(p1[...])
    ch[...] = high
    cl[...] = low
    met(2)
    greet(3)

    @pl.when(j > 0)
    def _():
        def pass_on(p, _):
            rows, copy = piece(p)
            copy.wait_recv()
            incoming = xt[rows, :]
            rest = incoming - incoming.astype(BF16).astype(F32)
            both = jnp.concatenate([incoming, rest], axis=0).astype(BF16)
            product = nn(both, ch[...]) + nn(both, cl[...])
            gt[2, rows] = lt[2, rows] + (product[:width] + product[width:])

            @pl.when(j < cuts - 1)
            def _():
                copy.start()

            return 0

        lax.fori_loop(0, PIECES, pass_on, 0)
        high, low = halves(xt[...])
        gt[0] = lt[0] + (nn(high, t0h[...]) + (nn(low, t0h[...]) + nn(high, t0l[...])))
        gt[1] = lt[1] + (nn(high, p1h[...]) + (nn(low, p1h[...]) + nn(high, p1l[...])))

    part[...] = jnp.zeros_like(part)
    for k in range(count):
        square = gt[k] * gt[k]
        total = jnp.sum(square, axis=0, keepdims=True)
        for i in range(strips):
            part[k * strips + i : k * strips + i + 1, :] = total[:, i * lanes : (i + 1) * lanes]
    sums = [remote(part, ga.at[r - 1], as_sem.at[r - 1], ar_sem.at[r - 1], along_group(r)) for r in range(1, groups)]
    for copy in sums:
        copy.start()
    for k in range(count):
        inner[k] = nn(gt[k].astype(BF16), coup[...])
    for copy in sums:
        copy.wait_recv()
    whole = part[...]
    for r in range(1, groups):
        whole = whole + ga[r - 1]
    n = count * strips
    ed[0] = whole[0:8]
    ed[1] = whole[n - 8 : n]
    down = remote(ed.at[0], er.at[1], es_sem.at[0], er_sem.at[1], along_z(-1))
    rise = remote(ed.at[1], er.at[0], es_sem.at[1], er_sem.at[0], along_z(1))

    @pl.when(j > 0)
    def _():
        down.start()

    @pl.when(j < cuts - 1)
    def _():
        rise.start()

    @pl.when(j == 0)
    def _():
        er[0] = jnp.zeros_like(er[0])

    @pl.when(j == cuts - 1)
    def _():
        er[1] = jnp.zeros_like(er[1])

    @pl.when(j > 0)
    def _():
        rise.wait_recv()

    @pl.when(j < cuts - 1)
    def _():
        down.wait_recv()

    left = jnp.concatenate([er[0, 8 - strips : 8], whole[0 : n - strips]], axis=0)
    right = jnp.concatenate([whole[strips:n], er[1, 0:strips]], axis=0)
    smb[...] = jnp.zeros_like(smb)
    smb[0:n] = whole[0:n] + 0.5 * (left + right)
    smooth = [remote(smb, ys.at[r - 1], ys_sem.at[r - 1], yr_sem.at[r - 1], along_y(r)) for r in range(1, ny)]
    for copy in smooth:
        copy.start()
    own = smb[...] * w[0:1, :]
    other = smb[...] * w[ny : ny + 1, :]
    for r in range(1, ny):
        smooth[r - 1].wait_recv()
        own = own + ys[r - 1] * w[r : r + 1, :]
        other = other + ys[r - 1] * w[ny + r : ny + r + 1, :]
    zs[...] = other
    met(3)
    across = remote(zs, zr, z_sem.at[0], z_sem.at[1], along_z(cuts))
    across.start()
    for k in range(count):
        gout[pl.ds(k * orbs, orbs), :] = gt[k].T
    stores = [local(gout, green.at[0], store.at[0])]
    stores[0].start()
    across.wait_recv()
    selfen = own + zr[...]
    for k in range(count):
        row = jnp.concatenate([selfen[k * strips + i : k * strips + i + 1, :] for i in range(strips)], axis=1)
        scaled = (inner[k] * row).astype(BF16)
        rows = pl.ds(k * orbs, orbs)
        sout[rows, :] = nt(coup[...], scaled)
        copy = local(sout.at[rows], scat.at[0, rows], store.at[k + 1])
        copy.start()
        stores.append(copy)

    @pl.when(j < cuts - 1)
    def _():
        def sent(p, _):
            piece(p)[1].wait_send()
            return 0

        lax.fori_loop(0, PIECES, sent, 0)
        rise.wait_send()

    @pl.when(j > 0)
    def _():
        down.wait_send()

    for copy in sums + smooth + [across]:
        copy.wait_send()
    for copy in stores:
        copy.wait()


def body(sizes, transfer, source, coupling, strength, mode_shift):
    cuts, energies, groups = sizes
    count, orbs = transfer.shape[1], transfer.shape[2]
    rows, cols = source.shape[1], source.shape[2]
    ny = energies // HALVES
    e = lax.axis_index("energy")
    y, half = e % ny, e // ny
    targets = jnp.stack([e, (e + ny) % energies])
    froms = half * ny + (y - jnp.arange(ny, dtype=jnp.int32)) % ny
    goal = (targets[:, None] + mode_shift[None, :]) % energies
    hits = goal[:, None, :] == froms[None, :, None]
    weights = jnp.sum(jnp.where(hits, strength[None, None, :], 0.0), axis=2) / (cols * groups)
    lanes = 128
    weights = jnp.broadcast_to(weights.reshape(2 * ny, 1), (2 * ny, lanes))
    vmem = pltpu.VMEM
    dma = pltpu.SemaphoreType.DMA
    small = 16
    any_space = pl.BlockSpec(memory_space=pl.ANY)
    in_vmem = pl.BlockSpec(memory_space=pltpu.VMEM)
    out = jax.ShapeDtypeStruct(source.shape, F32)
    return pl.pallas_call(
        functools.partial(kernel, (cuts, energies, groups, count)),
        out_shape=(out, out),
        in_specs=[any_space, any_space, in_vmem, in_vmem],
        out_specs=(any_space, any_space),
        scratch_shapes=[
            vmem((count, orbs, orbs), F32),
            vmem((rows, cols), F32),
            *[vmem((orbs, orbs), BF16) for _ in range(10)],
            vmem((orbs, orbs), F32),
            vmem((count, cols, orbs), F32),
            vmem((cols, orbs), F32),
            vmem((count, cols, orbs), F32),
            vmem((count, cols, orbs), F32),
            vmem((rows, cols), F32),
            vmem((rows, cols), F32),
            vmem((small, lanes), F32),
            vmem((groups - 1, small, lanes), F32),
            vmem((2, 8, lanes), F32),
            vmem((2, 8, lanes), F32),
            vmem((small, lanes), F32),
            vmem((ny - 1, small, lanes), F32),
            vmem((small, lanes), F32),
            vmem((small, lanes), F32),
            dma((count + 1,)),
            dma((count + 1,)),
            dma((PIECES,)),
            dma((PIECES,)),
            dma((groups - 1,)),
            dma((groups - 1,)),
            dma((2,)),
            dma((2,)),
            dma((ny - 1,)),
            dma((ny - 1,)),
            dma((2,)),
            pltpu.SemaphoreType.REGULAR((4,)),
            pltpu.SemaphoreType.REGULAR((4,)),
        ],
        compiler_params=pltpu.CompilerParams(collective_id=0, has_side_effects=True, vmem_limit_bytes=48 * 2**20),
        name="propagate_scatter",
    )(transfer, source, coupling, weights)


def solution(mesh):
    sizes = tuple(mesh.shape[name] for name in ("cuts", "energy", "group"))
    in_specs = (P("energy", "cuts", None, None), P("energy", "cuts", "group"), P(), P(), P())
    out_specs = (P("energy", "cuts", "group"), P("energy", "cuts", "group"))
    return jax.shard_map(functools.partial(body, sizes), mesh=mesh, in_specs=in_specs, out_specs=out_specs, check_vma=False)
```

time: 268 us -> 98.4 us (0.37)
  the two profiles are of different devices: /device:TPU:96 before, /device:TPU:448 now
where the time goes in v1:
time: 98.4 us; the launch traced here: 98.1 us
  Pallas kernels  89.8 us (91%)
  local copies, waits for them, and re-layouts  5.98 us (6%)
  other arithmetic  1.63 us (2%)
    pallas_call x1, Pallas kernels, body(): pl.pallas_call(functools.partial(kernel, (cuts, energies, groups, count))...  89.8 us
    unnamed x8, local copies, waits for them, and re-layouts  5.82 us

profile of v1, /device:TPU:448, one launch (start us, length us, event | category | flops | bytes accessed | tf_op | source)
XLA Modules:
  0.0 98.1 jit_solution(11107554193737403670)
XLA Ops:
  0.7 0.1 pad_add_fusion
  0.7 0.7 and_select_fusion.1
  1.5 0.8 select_reduce_fusion
  2.3 0.1 div.17
  2.4 0.1 broadcast_in_dim.24.w
  2.5 0.0 copy-start
  2.5 1.9 %copy-done = f32[1,3,512,512]{3,2,1,0:T(8,128)S(1)} copy-done((f32[1,3,512,512]{3,2,1,0:T(8,128)S(1)}, f32[1,3,512,512]{3,2,1,0:T(8,128)}, u32[]{:S(2)}) %copy-start) | copy-done | bytes 3145752
  4.3 0.0 copy-start.1
  4.3 1.1 %copy-done.1 = f32[1,1536,128]{2,1,0:T(8,128)S(1)} copy-done((f32[1,1536,128]{2,1,0:T(8,128)S(1)}, f32[1,1536,128]{2,1,0:T(8,128)}, u32[]{:S(2)}) %copy-start.1) | copy-done | bytes 786456
  5.5 0.0 copy-start.2
  5.5 1.0 %copy-done.2 = bf16[512,512]{1,0:T(8,128)(2,1)S(1)} copy-done((bf16[512,512]{1,0:T(8,128)(2,1)S(1)}, bf16[512,512]{1,0:T(8,128)(2,1)}, u32[]{:S(2)}) %copy-start.2) | copy-done | bytes 524312
  6.5 89.8 %propagate_scatter.1 = (f32[1,1536,128]{2,1,0:T(8,128)S(1)}, f32[1,1536,128]{2,1,0:T(8,128)S(1)}) custom-call(f32[1,3,512,512]{3,2,1,0:T(8,128)S(1)} %copy-done, f32[1,1536,128]{2,1,0:T(8,128)S(1)} %copy-done.1, bf16[512,512]{1,0:T(8,128)(2,1)S(1)} %copy-done.2, f32[8,128]{1,0:T(8,128)S(1)} %broadcast_in_dim.24.w), custom_call_target="tpu_custom_call" | custom-call | tf_op jit(solution)/shard_map/propagate_scatter/pallas_call | solution.py:269
  96.3 0.9 copy.9
  97.2 0.9 copy.10
  (2 shorter events, 0.0 us)
Async XLA Ops:
  2.5 1.9 %copy-start = (f32[1,3,512,512]{3,2,1,0:T(8,128)S(1)}, f32[1,3,512,512]{3,2,1,0:T(8,128)}, u32[]{:S(2)}) copy-start(f32[1,3,512,512]{3,2,1,0:T(8,128)} %t_hbm.1) | copy-start | bytes 9437188
  4.3 1.1 %copy-start.1 = (f32[1,1536,128]{2,1,0:T(8,128)S(1)}, f32[1,1536,128]{2,1,0:T(8,128)}, u32[]{:S(2)}) copy-start(f32[1,1536,128]{2,1,0:T(8,128)} %s_hbm.1) | copy-start | bytes 2359300
  5.5 1.0 %copy-start.2 = (bf16[512,512]{1,0:T(8,128)(2,1)S(1)}, bf16[512,512]{1,0:T(8,128)(2,1)}, u32[]{:S(2)}) copy-start(bf16[512,512]{1,0:T(8,128)(2,1)} %coup.1) | copy-start | bytes 1572868

commit v2 on v1

v2 whole, which is shorter than its diff:
```python
import functools

import jax
import jax.numpy as jnp
from jax import lax
from jax.experimental import pallas as pl
from jax.experimental.pallas import tpu as pltpu
from jax.sharding import PartitionSpec as P

MESH = pl.DeviceIdType.MESH
F32, BF16 = jnp.float32, jnp.bfloat16
PIECES = 16
HALVES = 2


def halves(value):
    high = value.astype(BF16)
    return high, (value - high.astype(F32)).astype(BF16)


def nn(left, right):
    return jnp.dot(left, right, preferred_element_type=F32)


def nt(left, right):
    return lax.dot_general(left, right, (((1,), (1,)), ((), ())), preferred_element_type=F32)


def kernel(sizes, t_hbm, s_hbm, c_hbm, strength, shift, gout, inner, sel, coup, tb, sb, ah, al, bh, bl, t0h, t0l, p1h, p1l, ch, cl,
           p1, lt, xt, gt, part, ga, ys, zs, zr, eds, edr, load, xs_sem, xr_sem, as_sem, ar_sem, ys_sem, yr_sem, z_sem, es_sem, er_sem,
           up_sem, dn_sem):
    cuts, energies, groups, count = sizes
    ny = energies // HALVES
    nz = HALVES * cuts
    j, e, q = lax.axis_index("cuts"), lax.axis_index("energy"), lax.axis_index("group")
    y = lax.rem(e, ny)
    z = (e // ny) * cuts + j
    orbs, cols = tb.shape[1], xt.shape[0]
    lanes = part.shape[1]
    strips = orbs // lanes
    width = cols // PIECES

    def along_z(step):
        there = lax.rem(z + step + nz, nz)
        return (lax.rem(there, cuts), (there // cuts) * ny + y, q)

    def along_group(step):
        return (j, e, lax.rem(q + step, groups))

    def along_y(step):
        return (j, (e // ny) * ny + lax.rem(y + step, ny), q)

    def local(src, dst, sem):
        return pltpu.make_async_copy(src, dst, sem)

    def remote(src, dst, send, recv, device):
        return pltpu.make_async_remote_copy(src_ref=src, dst_ref=dst, send_sem=send, recv_sem=recv, device_id=device, device_id_type=MESH)

    loads = [local(t_hbm.at[0, k], tb.at[k], load.at[k]) for k in range(count)]
    loads.append(local(s_hbm.at[0], sb, load.at[count]))
    loads.append(local(c_hbm, coup, load.at[count + 1]))
    for k in (count, *range(1, count), 0, count + 1):
        loads[k].start()

    barrier = pltpu.get_barrier_semaphore()
    near = [along_z(1), along_z(-1)] + [along_group(r) for r in range(1, groups)] + [along_y(r) for r in range(1, ny)]
    for device in near:
        pl.semaphore_signal(barrier, inc=1, device_id=device, device_id_type=MESH)
    pl.semaphore_wait(barrier, len(near))

    def greet(rnd):
        pl.semaphore_signal(up_sem.at[rnd], inc=1, device_id=along_z(2**rnd), device_id_type=MESH)
        pl.semaphore_signal(dn_sem.at[rnd], inc=1, device_id=along_z(-(2**rnd)), device_id_type=MESH)

    def met(rnd):
        pl.semaphore_wait(up_sem.at[rnd], 1)
        pl.semaphore_wait(dn_sem.at[rnd], 1)

    greet(0)

    def weight(target, source):
        total = 0.0
        for m in range(strength.shape[0]):
            total = total + jnp.where(lax.rem(target + shift[m], energies) == source, strength[m], 0.0)
        return total / (cols * groups)

    sources = [(e // ny) * ny + lax.rem(y - r + ny, ny) for r in range(ny)]
    w = [[weight(target, source) for source in sources] for target in (e, lax.rem(e + ny, energies))]

    loads[count].wait()
    for k in range(count):
        lt[k] = sb[pl.ds(k * orbs, orbs), :].T
    loads[1].wait()
    ah[...], al[...] = halves(tb[1])
    high, low = halves(lt[0])
    lt[1] = lt[1] + (nt(high, ah[...]) + (nt(low, ah[...]) + nt(high, al[...])))
    loads[2].wait()
    bh[...], bl[...] = halves(tb[2])
    high, low = halves(lt[1])
    lt[2] = lt[2] + (nt(high, bh[...]) + (nt(low, bh[...]) + nt(high, bl[...])))

    def piece(p):
        rows = pl.ds(pl.multiple_of(p * width, width), width)
        return rows, remote(gt.at[2, rows], xt.at[rows], xs_sem.at[p], xr_sem.at[p], along_z(1))

    @pl.when(j == 0)
    def _():
        gt[2] = lt[2]

        def send(p, _):
            piece(p)[1].start()
            return 0

        lax.fori_loop(0, PIECES, send, 0)
        gt[0] = lt[0]
        gt[1] = lt[1]

    met(0)
    greet(1)

    loads[0].wait()
    t0h[...], t0l[...] = halves(tb[0].T)
    p1[...] = nt(t0h[...], ah[...]) + (nt(t0l[...], ah[...]) + nt(t0h[...], al[...]))
    p1h[...], p1l[...] = halves(p1[...])
    met(1)
    greet(2)
    p1[...] = nt(p1h[...], bh[...]) + (nt(p1l[...], bh[...]) + nt(p1h[...], bl[...]))
    ch[...], cl[...] = halves(p1[...])
    met(2)
    greet(3)
    loads[count + 1].wait()

    @pl.when(j > 0)
    def _():
        def pass_on(p, _):
            rows, copy = piece(p)
            copy.wait_recv()
            incoming = xt[rows, :]
            rest = incoming - incoming.astype(BF16).astype(F32)
            both = jnp.concatenate([incoming, rest], axis=0).astype(BF16)
            product = nn(both, ch[...]) + nn(both, cl[...])
            gt[2, rows] = lt[2, rows] + (product[:width] + product[width:])

            @pl.when(j < cuts - 1)
            def _():
                copy.start()

            return 0

        lax.fori_loop(0, PIECES, pass_on, 0)
        high, low = halves(xt[...])
        gt[0] = lt[0] + (nn(high, t0h[...]) + (nn(low, t0h[...]) + nn(high, t0l[...])))
        gt[1] = lt[1] + (nn(high, p1h[...]) + (nn(low, p1h[...]) + nn(high, p1l[...])))

    part[...] = jnp.zeros_like(part)
    for k in range(count):
        square = gt[k] * gt[k]
        total = jnp.sum(square, axis=0, keepdims=True)
        for i in range(strips):
            part[k * strips + i : k * strips + i + 1, :] = total[:, i * lanes : (i + 1) * lanes]
    sums = [remote(part, ga.at[r - 1], as_sem.at[r - 1], ar_sem.at[r - 1], along_group(r)) for r in range(1, groups)]
    for copy in sums:
        copy.start()
    for k in range(count):
        inner[k] = nn(gt[k].astype(BF16), coup[...])
    for copy in sums:
        copy.wait_recv()
    whole = part[...]
    for r in range(1, groups):
        whole = whole + ga[r - 1]
    zs[2] = whole
    dense = [remote(zs.at[2], ys.at[r - 1], ys_sem.at[r - 1], yr_sem.at[r - 1], along_y(r)) for r in range(1, ny)]
    for copy in dense:
        copy.start()
    own = whole * w[0][0]
    other = whole * w[1][0]
    for k in range(count):
        gout[pl.ds(k * orbs, orbs), :] = gt[k].T
    for r in range(1, ny):
        dense[r - 1].wait_recv()
        own = own + ys[r - 1] * w[0][r]
        other = other + ys[r - 1] * w[1][r]
    n = count * strips
    zs[0] = other
    for t, value in enumerate((own, other)):
        eds[t, 0] = value[0:8]
        eds[t, 1] = value[n - 8 : n]
    met(3)
    across = remote(zs.at[0], zr, z_sem.at[0], z_sem.at[1], along_z(cuts))
    across.start()
    down = [remote(eds.at[t, 0], edr.at[t, 1], es_sem.at[t, 0], er_sem.at[t, 1], along_z(t * cuts - 1)) for t in (1, 0)]
    rise = [remote(eds.at[t, 1], edr.at[t, 0], es_sem.at[t, 1], er_sem.at[t, 0], along_z(t * cuts + 1)) for t in (1, 0)]

    @pl.when(j > 0)
    def _():
        for copy in down:
            copy.start()

    @pl.when(j < cuts - 1)
    def _():
        for copy in rise:
            copy.start()

    @pl.when(j == 0)
    def _():
        for t in (0, 1):
            edr[t, 0] = jnp.zeros_like(edr[t, 0])

    @pl.when(j == cuts - 1)
    def _():
        for t in (0, 1):
            edr[t, 1] = jnp.zeros_like(edr[t, 1])

    @pl.when(j > 0)
    def _():
        for copy in rise:
            copy.wait_recv()

    @pl.when(j < cuts - 1)
    def _():
        for copy in down:
            copy.wait_recv()

    across.wait_recv()
    total = own + zr[...]
    left = jnp.concatenate([edr[0, 0, 8 - strips : 8] + edr[1, 0, 8 - strips : 8], total[0 : n - strips]], axis=0)
    right = jnp.concatenate([total[strips:n], edr[0, 1, 0:strips] + edr[1, 1, 0:strips]], axis=0)
    sel[0:n] = total[0:n] + 0.5 * (left + right)

    @pl.when(j < cuts - 1)
    def _():
        def sent(p, _):
            piece(p)[1].wait_send()
            return 0

        lax.fori_loop(0, PIECES, sent, 0)
        for copy in rise:
            copy.wait_send()

    @pl.when(j > 0)
    def _():
        for copy in down:
            copy.wait_send()

    for copy in sums + dense + [across]:
        copy.wait_send()


def finish(gin, inner, sel, c_hbm, green, scat, coup, sout, sem):
    count, orbs, lanes = inner.shape[0], inner.shape[2], sel.shape[1]
    strips = orbs // lanes
    stores = [pltpu.make_async_copy(gin, green.at[0], sem.at[count])]
    stores[0].start()
    fetch = pltpu.make_async_copy(c_hbm, coup, sem.at[count + 1])
    fetch.start()
    fetch.wait()
    for k in range(count):
        row = jnp.concatenate([sel[k * strips + i : k * strips + i + 1, :] for i in range(strips)], axis=1)
        rows = pl.ds(k * orbs, orbs)
        sout[rows, :] = nt(coup[...], (inner[k] * row).astype(BF16))
        stores.append(pltpu.make_async_copy(sout.at[rows], scat.at[0, rows], sem.at[k]))
        stores[-1].start()
    for copy in stores:
        copy.wait()


def body(sizes, transfer, source, coupling, strength, mode_shift):
    cuts, energies, groups = sizes
    count, orbs = transfer.shape[1], transfer.shape[2]
    rows, cols = source.shape[1], source.shape[2]
    ny = energies // HALVES
    lanes = 128
    vmem = pltpu.VMEM
    dma = pltpu.SemaphoreType.DMA
    small = 16
    hbm = pl.BlockSpec(memory_space=pltpu.HBM)
    in_vmem = pl.BlockSpec(memory_space=pltpu.VMEM)
    scalars = pl.BlockSpec(memory_space=pltpu.SMEM)
    struct = jax.ShapeDtypeStruct
    coupled = [vmem((orbs, orbs), BF16)]
    green, inner, sel = pl.pallas_call(
        functools.partial(kernel, (cuts, energies, groups, count)),
        out_shape=(struct((rows, cols), F32), struct((count, cols, orbs), F32), struct((small, lanes), F32)),
        in_specs=[hbm, hbm, hbm, scalars, scalars],
        out_specs=(in_vmem, in_vmem, in_vmem),
        scratch_shapes=[
            *coupled,
            vmem((count, orbs, orbs), F32),
            vmem((rows, cols), F32),
            *[vmem((orbs, orbs), BF16) for _ in range(10)],
            vmem((orbs, orbs), F32),
            vmem((count, cols, orbs), F32),
            vmem((cols, orbs), F32),
            vmem((count, cols, orbs), F32),
            vmem((small, lanes), F32),
            vmem((groups - 1, small, lanes), F32),
            vmem((ny - 1, small, lanes), F32),
            vmem((3, small, lanes), F32),
            vmem((small, lanes), F32),
            vmem((2, 2, 8, lanes), F32),
            vmem((2, 2, 8, lanes), F32),
            dma((count + 2,)),
            dma((PIECES,)),
            dma((PIECES,)),
            dma((groups - 1,)),
            dma((groups - 1,)),
            dma((ny - 1,)),
            dma((ny - 1,)),
            dma((2,)),
            dma((2, 2)),
            dma((2, 2)),
            pltpu.SemaphoreType.REGULAR((4,)),
            pltpu.SemaphoreType.REGULAR((4,)),
        ],
        compiler_params=pltpu.CompilerParams(collective_id=0, has_side_effects=True, vmem_limit_bytes=54000000),
        name="propagate",
    )(transfer, source, coupling, strength, mode_shift)
    out = struct(source.shape, F32)
    return pl.pallas_call(
        finish,
        out_shape=(out, out),
        in_specs=[in_vmem, in_vmem, in_vmem, hbm],
        out_specs=(hbm, hbm),
        scratch_shapes=[*coupled, vmem((rows, cols), F32), dma((count + 2,))],
        compiler_params=pltpu.CompilerParams(vmem_limit_bytes=16 * 2**20),
        name="finish",
    )(green, inner, sel, coupling)


def solution(mesh):
    sizes = tuple(mesh.shape[name] for name in ("cuts", "energy", "group"))
    in_specs = (P("energy", "cuts", None, None), P("energy", "cuts", "group"), P(), P(), P())
    out_specs = (P("energy", "cuts", "group"), P("energy", "cuts", "group"))
    return jax.shard_map(functools.partial(body, sizes), mesh=mesh, in_specs=in_specs, out_specs=out_specs, check_vma=False)
```

time: 98.4 us -> 88.6 us (0.900)
  Pallas kernels: 89.8 us -> 85.4 us
  local copies, waits for them, and re-layouts: 5.98 us -> 2.34 us
  other arithmetic: 1.63 us -> 0 us
    pallas_call x1, Pallas kernels: 89.8 us -> 83.9 us  [body(): pl.pallas_call(functools.partial(kernel, (cuts, energies, groups, count))...]
    unnamed x8 -> x6, local copies, waits for them, and re-layouts: 5.82 us -> 2.34 us
    pallas_call x0 -> x1, Pallas kernels: none -> 1.45 us  [body(): pl.pallas_call(finish, out_shape=(out, out), in_specs=[in_vmem, in_vmem,...]
where the time goes in v2:
time: 88.6 us; the launch traced here: 88.4 us
  Pallas kernels  85.4 us (96%)
  local copies, waits for them, and re-layouts  2.34 us (3%)
    pallas_call x1, Pallas kernels, body(): pl.pallas_call(functools.partial(kernel, (cuts, energies, groups, count))...  83.9 us
    unnamed x6, local copies, waits for them, and re-layouts  2.34 us

profile of v2, /device:TPU:448, one launch (start us, length us, event | category | flops | bytes accessed | tf_op | source)
XLA Modules:
  0.0 88.4 jit_solution(6770830242596791413)
XLA Ops:
  0.6 0.0 copy-start
  0.6 1.0 %copy-done = bf16[512,512]{1,0:T(8,128)(2,1)S(1)} copy-done((bf16[512,512]{1,0:T(8,128)(2,1)S(1)}, bf16[512,512]{1,0:T(8,128)(2,1)}, u32[]{:S(2)}) %copy-start) | copy-done | bytes 524312
  1.7 0.0 copy-start.1
  1.7 0.7 copy-done.1
  2.3 0.0 copy-start.2
  2.3 0.7 copy-done.2
  3.0 83.9 %propagate.1 = (f32[1536,128]{1,0:T(8,128)S(1)}, f32[3,128,512]{2,1,0:T(8,128)S(1)}, f32[16,128]{1,0:T(8,128)S(1)}) custom-call(f32[1,3,512,512]{3,2,1,0:T(8,128)} %t_hbm.1, f32[1,1536,128]{2,1,0:T(8,128)} %s_hbm.1, bf16[512,512]{1,0:T(8,128)(2,1)S(1)} %copy-done, f32[8]{0:T(128)S(1)} %copy-done.1, s32[8]{0:T(128)S(1)} %copy-done.2), custom_call_target="tpu_custom_call" | custom-call | tf_op jit(solution)/shard_map/propagate/pallas_call | solution.py:281
  86.9 1.5 %finish.1 = (f32[1,1536,128]{2,1,0:T(8,128)}, f32[1,1536,128]{2,1,0:T(8,128)}) custom-call(f32[1536,128]{1,0:T(8,128)S(1)} %get-tuple-element.5.gin, f32[3,128,512]{2,1,0:T(8,128)S(1)} %get-tuple-element.6.inner, f32[16,128]{1,0:T(8,128)S(1)} %get-tuple-element.7.sel, bf16[512,512]{1,0:T(8,128)(2,1)S(1)} %copy-done), custom_call_target="tpu_custom_call" | custom-call | tf_op jit(solution)/shard_map/finish/pallas_call | solution.py:319
Async XLA Ops:
  0.6 1.0 %copy-start = (bf16[512,512]{1,0:T(8,128)(2,1)S(1)}, bf16[512,512]{1,0:T(8,128)(2,1)}, u32[]{:S(2)}) copy-start(bf16[512,512]{1,0:T(8,128)(2,1)} %c_hbm.3) | copy-start | bytes 1572868
  1.7 0.7 copy-start.1
  2.3 0.7 copy-start.2

commit v3 on v2

--- a/solution.py
+++ b/solution.py
@@ -26,7 +26,7 @@
     return lax.dot_general(left, right, (((1,), (1,)), ((), ())), preferred_element_type=F32)
 
 
-def kernel(sizes, t_hbm, s_hbm, c_hbm, strength, shift, gout, inner, sel, coup, tb, sb, ah, al, bh, bl, t0h, t0l, p1h, p1l, ch, cl,
+def kernel(sizes, t_hbm, s_hbm, c_hbm, strength_hbm, shift_hbm, gout, inner, sel, strength, shift, coup, tb, sb, ah, al, bh, bl, t0h, t0l, p1h, p1l, ch, cl,
            p1, lt, xt, gt, part, ga, ys, zs, zr, eds, edr, load, xs_sem, xr_sem, as_sem, ar_sem, ys_sem, yr_sem, z_sem, es_sem, er_sem,
            up_sem, dn_sem):
     cuts, energies, groups, count = sizes
@@ -59,7 +59,9 @@
     loads = [local(t_hbm.at[0, k], tb.at[k], load.at[k]) for k in range(count)]
     loads.append(local(s_hbm.at[0], sb, load.at[count]))
     loads.append(local(c_hbm, coup, load.at[count + 1]))
-    for k in (count, *range(1, count), 0, count + 1):
+    loads.append(local(strength_hbm, strength, load.at[count + 2]))
+    loads.append(local(shift_hbm, shift, load.at[count + 3]))
+    for k in (count, *range(1, count), 0, count + 1, count + 2, count + 3):
         loads[k].start()
 
     barrier = pltpu.get_barrier_semaphore()
@@ -77,15 +79,6 @@
         pl.semaphore_wait(dn_sem.at[rnd], 1)
 
     greet(0)
-
-    def weight(target, source):
-        total = 0.0
-        for m in range(strength.shape[0]):
-            total = total + jnp.where(lax.rem(target + shift[m], energies) == source, strength[m], 0.0)
-        return total / (cols * groups)
-
-    sources = [(e // ny) * ny + lax.rem(y - r + ny, ny) for r in range(ny)]
-    w = [[weight(target, source) for source in sources] for target in (e, lax.rem(e + ny, energies))]
 
     loads[count].wait()
     for k in range(count):
@@ -126,8 +119,11 @@
     greet(2)
     p1[...] = nt(p1h[...], bh[...]) + (nt(p1l[...], bh[...]) + nt(p1h[...], bl[...]))
     ch[...], cl[...] = halves(p1[...])
-    met(2)
-    greet(3)
+    @pl.when(j >= 4)
+    def _():
+        met(2)
+        greet(3)
+
     loads[count + 1].wait()
 
     @pl.when(j > 0)
@@ -152,6 +148,11 @@
         gt[0] = lt[0] + (nn(high, t0h[...]) + (nn(low, t0h[...]) + nn(high, t0l[...])))
         gt[1] = lt[1] + (nn(high, p1h[...]) + (nn(low, p1h[...]) + nn(high, p1l[...])))
 
+    @pl.when(j < 4)
+    def _():
+        met(2)
+        greet(3)
+
     part[...] = jnp.zeros_like(part)
     for k in range(count):
         square = gt[k] * gt[k]
@@ -163,6 +164,18 @@
         copy.start()
     for k in range(count):
         inner[k] = nn(gt[k].astype(BF16), coup[...])
+    loads[count + 2].wait()
+    loads[count + 3].wait()
+
+    def weight(target, source):
+        total = 0.0
+        for m in range(strength.shape[0]):
+            total = total + jnp.where(lax.rem(target + shift[m], energies) == source, strength[m], 0.0)
+        return total / (cols * groups)
+
+    sources = [(e // ny) * ny + lax.rem(y - r + ny, ny) for r in range(ny)]
+    w = [[weight(target, source) for source in sources] for target in (e, lax.rem(e + ny, energies))]
+
     for copy in sums:
         copy.wait_recv()
     whole = part[...]
@@ -275,15 +288,16 @@
     small = 16
     hbm = pl.BlockSpec(memory_space=pltpu.HBM)
     in_vmem = pl.BlockSpec(memory_space=pltpu.VMEM)
-    scalars = pl.BlockSpec(memory_space=pltpu.SMEM)
     struct = jax.ShapeDtypeStruct
     coupled = [vmem((orbs, orbs), BF16)]
     green, inner, sel = pl.pallas_call(
         functools.partial(kernel, (cuts, energies, groups, count)),
         out_shape=(struct((rows, cols), F32), struct((count, cols, orbs), F32), struct((small, lanes), F32)),
-        in_specs=[hbm, hbm, hbm, scalars, scalars],
+        in_specs=[hbm] * 5,
         out_specs=(in_vmem, in_vmem, in_vmem),
         scratch_shapes=[
+            pltpu.SMEM(strength.shape, F32),
+            pltpu.SMEM(mode_shift.shape, jnp.int32),
             *coupled,
             vmem((count, orbs, orbs), F32),
             vmem((rows, cols), F32),
@@ -299,7 +313,7 @@
             vmem((small, lanes), F32),
             vmem((2, 2, 8, lanes), F32),
             vmem((2, 2, 8, lanes), F32),
-            dma((count + 2,)),
+            dma((count + 4,)),
             dma((PIECES,)),
             dma((PIECES,)),
             dma((groups - 1,)),
@@ -314,7 +328,7 @@
         ],
         compiler_params=pltpu.CompilerParams(collective_id=0, has_side_effects=True, vmem_limit_bytes=54000000),
         name="propagate",
-    )(transfer, source, coupling, strength, mode_shift)
+    )(*[pltpu.with_memory_space_constraint(a, pltpu.HBM) for a in (transfer, source, coupling, strength, mode_shift)])
     out = struct(source.shape, F32)
     return pl.pallas_call(
         finish,

time: 88.6 us -> 83.7 us (0.945)
  Pallas kernels: 85.4 us -> 82.9 us
  local copies, waits for them, and re-layouts: 2.34 us -> 0.01 us
    pallas_call x1, Pallas kernels: 83.9 us -> 81.4 us  [body(): pl.pallas_call(functools.partial(kernel, (cuts, energies, groups, count))...]
    unnamed x6 -> x2, local copies, waits for them, and re-layouts: 2.34 us -> 0.01 us
where the time goes in v3:
time: 83.7 us; the launch traced here: 83.5 us
  Pallas kernels  82.9 us (99%)
    pallas_call x1, Pallas kernels, body(): pl.pallas_call(functools.partial(kernel, (cuts, energies, groups, count))...  81.4 us

profile of v3, /device:TPU:448, one launch (start us, length us, event | category | flops | bytes accessed | tf_op | source)
XLA Modules:
  0.0 83.5 jit_solution(8673566503874988827)
XLA Ops:
  0.6 0.0 copy-start
  0.6 81.4 %propagate.1 = (f32[1536,128]{1,0:T(8,128)S(1)}, f32[3,128,512]{2,1,0:T(8,128)S(1)}, f32[16,128]{1,0:T(8,128)S(1)}) custom-call(f32[1,3,512,512]{3,2,1,0:T(8,128)} %t_hbm.1, f32[1,1536,128]{2,1,0:T(8,128)} %s_hbm.1, bf16[512,512]{1,0:T(8,128)(2,1)} %c_hbm.3, f32[8]{0:T(128)} %strength_hbm.1, s32[8]{0:T(128)} %shift_hbm.1), custom_call_target="tpu_custom_call" | custom-call | tf_op jit(solution)/shard_map/propagate/pallas_call | solution.py:293
  82.1 0.0 copy-done
  82.1 1.4 %finish.1 = (f32[1,1536,128]{2,1,0:T(8,128)}, f32[1,1536,128]{2,1,0:T(8,128)}) custom-call(f32[1536,128]{1,0:T(8,128)S(1)} %get-tuple-element.5.gin, f32[3,128,512]{2,1,0:T(8,128)S(1)} %get-tuple-element.6.inner, f32[16,128]{1,0:T(8,128)S(1)} %get-tuple-element.7.sel, bf16[512,512]{1,0:T(8,128)(2,1)S(1)} %copy-done), custom_call_target="tpu_custom_call" | custom-call | tf_op jit(solution)/shard_map/finish/pallas_call | solution.py:333
Async XLA Ops:
  0.6 81.4 %copy-start = (bf16[512,512]{1,0:T(8,128)(2,1)S(1)}, bf16[512,512]{1,0:T(8,128)(2,1)}, u32[]{:S(2)}) copy-start(bf16[512,512]{1,0:T(8,128)(2,1)} %c_hbm.3) | copy-start | bytes 1572868

commit v4 on v3

--- a/solution.py
+++ b/solution.py
@@ -11,6 +11,7 @@
 F32, BF16 = jnp.float32, jnp.bfloat16
 PIECES = 16
 HALVES = 2
+FIRST = 7
 
 
 def halves(value):
@@ -27,8 +28,8 @@
 
 
 def kernel(sizes, t_hbm, s_hbm, c_hbm, strength_hbm, shift_hbm, gout, inner, sel, strength, shift, coup, tb, sb, ah, al, bh, bl, t0h, t0l, p1h, p1l, ch, cl,
-           p1, lt, xt, gt, part, ga, ys, zs, zr, eds, edr, load, xs_sem, xr_sem, as_sem, ar_sem, ys_sem, yr_sem, z_sem, es_sem, er_sem,
-           up_sem, dn_sem):
+           p1, cin, cih, cil, oin, lt, xt, gt, part, ga, ys, zs, zr, eds, edr, load, xs_sem, xr_sem, as_sem, ar_sem, ys_sem, yr_sem, z_sem, es_sem, er_sem,
+           cs_sem, cr_sem, ps_sem, pr_sem, ls_sem, up_sem, dn_sem):
     cuts, energies, groups, count = sizes
     ny = energies // HALVES
     nz = HALVES * cuts
@@ -39,6 +40,13 @@
     lanes = part.shape[1]
     strips = orbs // lanes
     width = cols // PIECES
+    core = lax.rem(q, 2)
+    odd = lax.rem(j, 2)
+    skips = (odd == 1) & (j >= FIRST) & (j < cuts - 4)
+    fed = (odd == 1) & (j > FIRST) & (j < cuts - 2)
+    feeds = (odd == 0) & (j > FIRST) & (j < cuts - 3)
+    passes = (j < cuts - 1) & jnp.logical_not(feeds)
+    at_once = passes & jnp.logical_not(skips)
 
     def along_z(step):
         there = lax.rem(z + step + nz, nz)
@@ -96,6 +104,22 @@
         rows = pl.ds(pl.multiple_of(p * width, width), width)
         return rows, remote(gt.at[2, rows], xt.at[rows], xs_sem.at[p], xr_sem.at[p], along_z(1))
 
+    def leap(p):
+        rows = pl.ds(pl.multiple_of(p * width, width), width)
+        return remote(gt.at[2, rows], xt.at[rows], ls_sem.at[p], xr_sem.at[p], along_z(2))
+
+    def quarter(half, i):
+        size = orbs // 4
+        return pl.ds(pl.multiple_of((2 * half + i) * size, size), size)
+
+    def share(half):
+        rows = [quarter(half, i) for i in range(2)]
+        partner = (j, e, q + 1 - 2 * core)
+        return [remote(cin.at[rows[i]], cin.at[rows[i]], ps_sem.at[i], pr_sem.at[i], partner) for i in range(2)]
+
+    feed = [remote(p1.at[quarter(core, i)], cin.at[quarter(core, i)], cs_sem.at[i], cr_sem.at[i], along_z(1)) for i in range(2)]
+    feed.append(remote(lt.at[2], oin, cs_sem.at[2], cr_sem.at[2], along_z(1)))
+
     @pl.when(j == 0)
     def _():
         gt[2] = lt[2]
@@ -119,12 +143,32 @@
     greet(2)
     p1[...] = nt(p1h[...], bh[...]) + (nt(p1l[...], bh[...]) + nt(p1h[...], bl[...]))
     ch[...], cl[...] = halves(p1[...])
+    @pl.when(feeds)
+    def _():
+        for copy in feed:
+            copy.start()
+
     @pl.when(j >= 4)
     def _():
         met(2)
         greet(3)
 
     loads[count + 1].wait()
+
+    @pl.when(fed)
+    def _():
+        given = share(core)
+        for i in range(2):
+            feed[i].wait_recv()
+            given[i].start()
+        feed[2].wait_recv()
+        high, low = halves(oin[...])
+        lt[2] = lt[2] + (nn(high, ch[...]) + (nn(low, ch[...]) + nn(high, cl[...])))
+        for copy in share(1 - core):
+            copy.wait_recv()
+        cih[...], cil[...] = halves(cin[...])
+        p1[...] = nn(cih[...], ch[...]) + (nn(cil[...], ch[...]) + nn(cih[...], cl[...]))
+        ch[...], cl[...] = halves(p1[...])
 
     @pl.when(j > 0)
     def _():
@@ -137,13 +181,31 @@
             product = nn(both, ch[...]) + nn(both, cl[...])
             gt[2, rows] = lt[2, rows] + (product[:width] + product[width:])
 
-            @pl.when(j < cuts - 1)
+            @pl.when(skips)
+            def _():
+                leap(p).start()
+
+            @pl.when(at_once)
             def _():
                 copy.start()
 
             return 0
 
         lax.fori_loop(0, PIECES, pass_on, 0)
+
+        @pl.when(skips)
+        def _():
+            def late(p, _):
+                piece(p)[1].start()
+                return 0
+
+            lax.fori_loop(0, PIECES, late, 0)
+
+        @pl.when(fed)
+        def _():
+            high, low = halves(xt[...])
+            xt[...] = oin[...] + (nn(high, cih[...]) + (nn(low, cih[...]) + nn(high, cil[...])))
+
         high, low = halves(xt[...])
         gt[0] = lt[0] + (nn(high, t0h[...]) + (nn(low, t0h[...]) + nn(high, t0l[...])))
         gt[1] = lt[1] + (nn(high, p1h[...]) + (nn(low, p1h[...]) + nn(high, p1l[...])))
@@ -240,13 +302,34 @@
     right = jnp.concatenate([total[strips:n], edr[0, 1, 0:strips] + edr[1, 1, 0:strips]], axis=0)
     sel[0:n] = total[0:n] + 0.5 * (left + right)
 
-    @pl.when(j < cuts - 1)
+    @pl.when(passes)
     def _():
         def sent(p, _):
             piece(p)[1].wait_send()
             return 0
 
         lax.fori_loop(0, PIECES, sent, 0)
+
+    @pl.when(skips)
+    def _():
+        def sent(p, _):
+            leap(p).wait_send()
+            return 0
+
+        lax.fori_loop(0, PIECES, sent, 0)
+
+    @pl.when(feeds)
+    def _():
+        for copy in feed:
+            copy.wait_send()
+
+    @pl.when(fed)
+    def _():
+        for copy in share(core):
+            copy.wait_send()
+
+    @pl.when(j < cuts - 1)
+    def _():
         for copy in rise:
             copy.wait_send()
 
@@ -303,6 +386,10 @@
             vmem((rows, cols), F32),
             *[vmem((orbs, orbs), BF16) for _ in range(10)],
             vmem((orbs, orbs), F32),
+            vmem((orbs, orbs), F32),
+            vmem((orbs, orbs), BF16),
+            vmem((orbs, orbs), BF16),
+            vmem((cols, orbs), F32),
             vmem((count, cols, orbs), F32),
             vmem((cols, orbs), F32),
             vmem((count, cols, orbs), F32),
@@ -323,6 +410,11 @@
             dma((2,)),
             dma((2, 2)),
             dma((2, 2)),
+            dma((3,)),
+            dma((3,)),
+            dma((2,)),
+            dma((2,)),
+            dma((PIECES,)),
             pltpu.SemaphoreType.REGULAR((4,)),
             pltpu.SemaphoreType.REGULAR((4,)),
         ],

time: 83.7 us -> 78 us (0.932)
  the two profiles are of different devices: /device:TPU:448 before, /device:TPU:352 now
where the time goes in v4:
time: 78 us; the launch traced here: 77.8 us
  Pallas kernels  77.2 us (99%)
    pallas_call x1, Pallas kernels, body(): pl.pallas_call(functools.partial(kernel, (cuts, energies, groups, count))...  75.7 us

profile of v4, /device:TPU:352, one launch (start us, length us, event | category | flops | bytes accessed | tf_op | source)
XLA Modules:
  0.0 77.8 jit_solution(7419677227363550007)
XLA Ops:
  0.6 0.0 copy-start
  0.6 75.7 %propagate.1 = (f32[1536,128]{1,0:T(8,128)S(1)}, f32[3,128,512]{2,1,0:T(8,128)S(1)}, f32[16,128]{1,0:T(8,128)S(1)}) custom-call(f32[1,3,512,512]{3,2,1,0:T(8,128)} %t_hbm.1, f32[1,1536,128]{2,1,0:T(8,128)} %s_hbm.1, bf16[512,512]{1,0:T(8,128)(2,1)} %c_hbm.3, f32[8]{0:T(128)} %strength_hbm.1, s32[8]{0:T(128)} %shift_hbm.1), custom_call_target="tpu_custom_call" | custom-call | tf_op jit(solution)/shard_map/propagate/pallas_call | solution.py:376
  76.4 0.0 copy-done
  76.4 1.4 %finish.1 = (f32[1,1536,128]{2,1,0:T(8,128)}, f32[1,1536,128]{2,1,0:T(8,128)}) custom-call(f32[1536,128]{1,0:T(8,128)S(1)} %get-tuple-element.5.gin, f32[3,128,512]{2,1,0:T(8,128)S(1)} %get-tuple-element.6.inner, f32[16,128]{1,0:T(8,128)S(1)} %get-tuple-element.7.sel, bf16[512,512]{1,0:T(8,128)(2,1)S(1)} %copy-done), custom_call_target="tpu_custom_call" | custom-call | tf_op jit(solution)/shard_map/finish/pallas_call | solution.py:425
Async XLA Ops:
  0.6 75.8 %copy-start = (bf16[512,512]{1,0:T(8,128)(2,1)S(1)}, bf16[512,512]{1,0:T(8,128)(2,1)}, u32[]{:S(2)}) copy-start(bf16[512,512]{1,0:T(8,128)(2,1)} %c_hbm.3) | copy-start | bytes 1572868

commit v5 on v4

--- a/solution.py
+++ b/solution.py
@@ -28,7 +28,7 @@
 
 
 def kernel(sizes, t_hbm, s_hbm, c_hbm, strength_hbm, shift_hbm, gout, inner, sel, strength, shift, coup, tb, sb, ah, al, bh, bl, t0h, t0l, p1h, p1l, ch, cl,
-           p1, cin, cih, cil, oin, lt, xt, gt, part, ga, ys, zs, zr, eds, edr, load, xs_sem, xr_sem, as_sem, ar_sem, ys_sem, yr_sem, z_sem, es_sem, er_sem,
+           p1, cin, cih, cil, oin, lt, xt, gt, part, ga, ys, zs, zr, eds, edr, edf, load, xs_sem, xr_sem, as_sem, ar_sem, ys_sem, yr_sem, zx_sem, zy_sem, es_sem, er_sem, fs_sem, fr_sem,
            cs_sem, cr_sem, ps_sem, pr_sem, ls_sem, up_sem, dn_sem):
     cuts, energies, groups, count = sizes
     ny = energies // HALVES
@@ -48,9 +48,9 @@
     passes = (j < cuts - 1) & jnp.logical_not(feeds)
     at_once = passes & jnp.logical_not(skips)
 
-    def along_z(step):
+    def along_z(step, turn=0):
         there = lax.rem(z + step + nz, nz)
-        return (lax.rem(there, cuts), (there // cuts) * ny + y, q)
+        return (lax.rem(there, cuts), (there // cuts) * ny + lax.rem(y + turn, ny), q)
 
     def along_group(step):
         return (j, e, lax.rem(q + step, groups))
@@ -79,8 +79,9 @@
     pl.semaphore_wait(barrier, len(near))
 
     def greet(rnd):
-        pl.semaphore_signal(up_sem.at[rnd], inc=1, device_id=along_z(2**rnd), device_id_type=MESH)
-        pl.semaphore_signal(dn_sem.at[rnd], inc=1, device_id=along_z(-(2**rnd)), device_id_type=MESH)
+        reach = 2 ** max(rnd - 1, 0)
+        pl.semaphore_signal(up_sem.at[rnd], inc=1, device_id=along_z(reach), device_id_type=MESH)
+        pl.semaphore_signal(dn_sem.at[rnd], inc=1, device_id=along_z(-reach), device_id_type=MESH)
 
     def met(rnd):
         pl.semaphore_wait(up_sem.at[rnd], 1)
@@ -91,6 +92,8 @@
     loads[count].wait()
     for k in range(count):
         lt[k] = sb[pl.ds(k * orbs, orbs), :].T
+    met(0)
+    greet(1)
     loads[1].wait()
     ah[...], al[...] = halves(tb[1])
     high, low = halves(lt[0])
@@ -132,15 +135,15 @@
         gt[0] = lt[0]
         gt[1] = lt[1]
 
-    met(0)
-    greet(1)
+    met(1)
+    greet(2)
 
     loads[0].wait()
     t0h[...], t0l[...] = halves(tb[0].T)
     p1[...] = nt(t0h[...], ah[...]) + (nt(t0l[...], ah[...]) + nt(t0h[...], al[...]))
     p1h[...], p1l[...] = halves(p1[...])
-    met(1)
-    greet(2)
+    met(2)
+    greet(3)
     p1[...] = nt(p1h[...], bh[...]) + (nt(p1l[...], bh[...]) + nt(p1h[...], bl[...]))
     ch[...], cl[...] = halves(p1[...])
     @pl.when(feeds)
@@ -150,8 +153,8 @@
 
     @pl.when(j >= 4)
     def _():
-        met(2)
-        greet(3)
+        met(3)
+        greet(4)
 
     loads[count + 1].wait()
 
@@ -212,8 +215,8 @@
 
     @pl.when(j < 4)
     def _():
-        met(2)
-        greet(3)
+        met(3)
+        greet(4)
 
     part[...] = jnp.zeros_like(part)
     for k in range(count):
@@ -235,56 +238,67 @@
             total = total + jnp.where(lax.rem(target + shift[m], energies) == source, strength[m], 0.0)
         return total / (cols * groups)
 
-    sources = [(e // ny) * ny + lax.rem(y - r + ny, ny) for r in range(ny)]
-    w = [[weight(target, source) for source in sources] for target in (e, lax.rem(e + ny, energies))]
-
+    below = [lax.rem(y - r + ny, ny) for r in range(ny)]
+    w = [[weight(e, half * ny + place) for place in below] for half in (e // ny, 1 - e // ny)]
     for copy in sums:
         copy.wait_recv()
     whole = part[...]
     for r in range(1, groups):
         whole = whole + ga[r - 1]
-    zs[2] = whole
-    dense = [remote(zs.at[2], ys.at[r - 1], ys_sem.at[r - 1], yr_sem.at[r - 1], along_y(r)) for r in range(1, ny)]
+    n = count * strips
+    zs[...] = whole
+    eds[1, 0] = whole[0:8]
+    eds[1, 1] = whole[n - 8 : n]
+    met(4)
+    across = [remote(zs, zr.at[r], zx_sem.at[r], zy_sem.at[r], along_z(cuts, r)) for r in range(ny)]
+    for copy in across:
+        copy.start()
+    down = [remote(eds.at[1, 0], edf.at[r, 1], fs_sem.at[r, 0], fr_sem.at[r, 1], along_z(cuts - 1, r)) for r in range(ny)]
+    rise = [remote(eds.at[1, 1], edf.at[r, 0], fs_sem.at[r, 1], fr_sem.at[r, 0], along_z(cuts + 1, r)) for r in range(ny)]
+    down.append(remote(eds.at[0, 0], edr.at[1], es_sem.at[0], er_sem.at[1], along_z(-1)))
+    rise.append(remote(eds.at[0, 1], edr.at[0], es_sem.at[1], er_sem.at[0], along_z(1)))
+
+    @pl.when(j > 0)
+    def _():
+        for copy in down[:ny]:
+            copy.start()
+
+    @pl.when(j < cuts - 1)
+    def _():
+        for copy in rise[:ny]:
+            copy.start()
+
+    dense = [remote(zs, ys.at[r - 1], ys_sem.at[r - 1], yr_sem.at[r - 1], along_y(r)) for r in range(1, ny)]
     for copy in dense:
         copy.start()
-    own = whole * w[0][0]
-    other = whole * w[1][0]
     for k in range(count):
         gout[pl.ds(k * orbs, orbs), :] = gt[k].T
+    own = whole * w[0][0]
     for r in range(1, ny):
         dense[r - 1].wait_recv()
         own = own + ys[r - 1] * w[0][r]
-        other = other + ys[r - 1] * w[1][r]
-    n = count * strips
-    zs[0] = other
-    for t, value in enumerate((own, other)):
-        eds[t, 0] = value[0:8]
-        eds[t, 1] = value[n - 8 : n]
-    met(3)
-    across = remote(zs.at[0], zr, z_sem.at[0], z_sem.at[1], along_z(cuts))
-    across.start()
-    down = [remote(eds.at[t, 0], edr.at[t, 1], es_sem.at[t, 0], er_sem.at[t, 1], along_z(t * cuts - 1)) for t in (1, 0)]
-    rise = [remote(eds.at[t, 1], edr.at[t, 0], es_sem.at[t, 1], er_sem.at[t, 0], along_z(t * cuts + 1)) for t in (1, 0)]
+    eds[0, 0] = own[0:8]
+    eds[0, 1] = own[n - 8 : n]
 
     @pl.when(j > 0)
     def _():
-        for copy in down:
-            copy.start()
+        down[ny].start()
 
     @pl.when(j < cuts - 1)
     def _():
-        for copy in rise:
-            copy.start()
+        rise[ny].start()
 
     @pl.when(j == 0)
     def _():
-        for t in (0, 1):
-            edr[t, 0] = jnp.zeros_like(edr[t, 0])
+        edr[0] = jnp.zeros_like(edr[0])
+        for r in range(ny):
+            edf[r, 0] = jnp.zeros_like(edf[r, 0])
 
     @pl.when(j == cuts - 1)
     def _():
-        for t in (0, 1):
-            edr[t, 1] = jnp.zeros_like(edr[t, 1])
+        edr[1] = jnp.zeros_like(edr[1])
+        for r in range(ny):
+            edf[r, 1] = jnp.zeros_like(edf[r, 1])
 
     @pl.when(j > 0)
     def _():
@@ -296,10 +310,15 @@
         for copy in down:
             copy.wait_recv()
 
-    across.wait_recv()
-    total = own + zr[...]
-    left = jnp.concatenate([edr[0, 0, 8 - strips : 8] + edr[1, 0, 8 - strips : 8], total[0 : n - strips]], axis=0)
-    right = jnp.concatenate([total[strips:n], edr[0, 1, 0:strips] + edr[1, 1, 0:strips]], axis=0)
+    before, after = edr[0], edr[1]
+    total = own
+    for r in range(ny):
+        across[r].wait_recv()
+        total = total + zr[r] * w[1][r]
+        before = before + edf[r, 0] * w[1][r]
+        after = after + edf[r, 1] * w[1][r]
+    left = jnp.concatenate([before[8 - strips : 8], total[0 : n - strips]], axis=0)
+    right = jnp.concatenate([total[strips:n], after[0:strips]], axis=0)
     sel[0:n] = total[0:n] + 0.5 * (left + right)
 
     @pl.when(passes)
@@ -338,18 +357,15 @@
         for copy in down:
             copy.wait_send()
 
-    for copy in sums + dense + [across]:
+    for copy in sums + dense + across:
         copy.wait_send()
 
 
-def finish(gin, inner, sel, c_hbm, green, scat, coup, sout, sem):
+def finish(gin, inner, sel, coup, green, scat, sout, sem):
     count, orbs, lanes = inner.shape[0], inner.shape[2], sel.shape[1]
     strips = orbs // lanes
     stores = [pltpu.make_async_copy(gin, green.at[0], sem.at[count])]
     stores[0].start()
-    fetch = pltpu.make_async_copy(c_hbm, coup, sem.at[count + 1])
-    fetch.start()
-    fetch.wait()
     for k in range(count):
         row = jnp.concatenate([sel[k * strips + i : k * strips + i + 1, :] for i in range(strips)], axis=1)
         rows = pl.ds(k * orbs, orbs)
@@ -396,10 +412,11 @@
             vmem((small, lanes), F32),
             vmem((groups - 1, small, lanes), F32),
             vmem((ny - 1, small, lanes), F32),
-            vmem((3, small, lanes), F32),
             vmem((small, lanes), F32),
+            vmem((ny, small, lanes), F32),
             vmem((2, 2, 8, lanes), F32),
-            vmem((2, 2, 8, lanes), F32),
+            vmem((2, 8, lanes), F32),
+            vmem((ny, 2, 8, lanes), F32),
             dma((count + 4,)),
             dma((PIECES,)),
             dma((PIECES,)),
@@ -407,16 +424,19 @@
             dma((groups - 1,)),
             dma((ny - 1,)),
             dma((ny - 1,)),
+            dma((ny,)),
+            dma((ny,)),
             dma((2,)),
-            dma((2, 2)),
-            dma((2, 2)),
+            dma((2,)),
+            dma((ny, 2)),
+            dma((ny, 2)),
             dma((3,)),
             dma((3,)),
             dma((2,)),
             dma((2,)),
             dma((PIECES,)),
-            pltpu.SemaphoreType.REGULAR((4,)),
-            pltpu.SemaphoreType.REGULAR((4,)),
+            pltpu.SemaphoreType.REGULAR((5,)),
+            pltpu.SemaphoreType.REGULAR((5,)),
         ],
         compiler_params=pltpu.CompilerParams(collective_id=0, has_side_effects=True, vmem_limit_bytes=54000000),
         name="propagate",
@@ -425,9 +445,9 @@
     return pl.pallas_call(
         finish,
         out_shape=(out, out),
-        in_specs=[in_vmem, in_vmem, in_vmem, hbm],
+        in_specs=[in_vmem] * 4,
         out_specs=(hbm, hbm),
-        scratch_shapes=[*coupled, vmem((rows, cols), F32), dma((count + 2,))],
+        scratch_shapes=[vmem((rows, cols), F32), dma((count + 1,))],
         compiler_params=pltpu.CompilerParams(vmem_limit_bytes=16 * 2**20),
         name="finish",
     )(green, inner, sel, coupling)

time: 78 us -> 81.6 us (1.046)
  the two profiles are of different devices: /device:TPU:352 before, /device:TPU:452 now
where the time goes in v5:
time: 81.6 us; the launch traced here: 81.4 us
  Pallas kernels  80.8 us (99%)
    pallas_call x1, Pallas kernels, body(): pl.pallas_call(functools.partial(kernel, (cuts, energies, groups, count))...  79.4 us

profile of v5, /device:TPU:452, one launch (start us, length us, event | category | flops | bytes accessed | tf_op | source)
XLA Modules:
  0.0 81.4 jit_solution(8156224743574296085)
XLA Ops:
  0.6 0.0 copy-start
  0.6 79.4 %propagate.1 = (f32[1536,128]{1,0:T(8,128)S(1)}, f32[3,128,512]{2,1,0:T(8,128)S(1)}, f32[16,128]{1,0:T(8,128)S(1)}) custom-call(f32[1,3,512,512]{3,2,1,0:T(8,128)} %t_hbm.1, f32[1,1536,128]{2,1,0:T(8,128)} %s_hbm.1, bf16[512,512]{1,0:T(8,128)(2,1)} %coup.1, f32[8]{0:T(128)} %strength_hbm.1, s32[8]{0:T(128)} %shift_hbm.1), custom_call_target="tpu_custom_call" | custom-call | tf_op jit(solution)/shard_map/propagate/pallas_call | solution.py:392
  80.0 0.0 copy-done
  80.0 1.4 %finish.1 = (f32[1,1536,128]{2,1,0:T(8,128)}, f32[1,1536,128]{2,1,0:T(8,128)}) custom-call(f32[1536,128]{1,0:T(8,128)S(1)} %get-tuple-element.5.gin, f32[3,128,512]{2,1,0:T(8,128)S(1)} %get-tuple-element.6.inner, f32[16,128]{1,0:T(8,128)S(1)} %get-tuple-element.7.sel, bf16[512,512]{1,0:T(8,128)(2,1)S(1)} %copy-done), custom_call_target="tpu_custom_call" | custom-call | tf_op jit(solution)/shard_map/finish/pallas_call | solution.py:445
Async XLA Ops:
  0.6 79.4 %copy-start = (bf16[512,512]{1,0:T(8,128)(2,1)S(1)}, bf16[512,512]{1,0:T(8,128)(2,1)}, u32[]{:S(2)}) copy-start(bf16[512,512]{1,0:T(8,128)(2,1)} %coup.1) | copy-start | bytes 1572868

commit v6 on v4

--- a/solution.py
+++ b/solution.py
@@ -215,7 +215,6 @@
         met(2)
         greet(3)
 
-    part[...] = jnp.zeros_like(part)
     for k in range(count):
         square = gt[k] * gt[k]
         total = jnp.sum(square, axis=0, keepdims=True)
@@ -258,8 +257,8 @@
     n = count * strips
     zs[0] = other
     for t, value in enumerate((own, other)):
-        eds[t, 0] = value[0:8]
-        eds[t, 1] = value[n - 8 : n]
+        eds[t, 0] = value[0:strips]
+        eds[t, 1] = value[n - strips : n]
     met(3)
     across = remote(zs.at[0], zr, z_sem.at[0], z_sem.at[1], along_z(cuts))
     across.start()
@@ -298,8 +297,8 @@
 
     across.wait_recv()
     total = own + zr[...]
-    left = jnp.concatenate([edr[0, 0, 8 - strips : 8] + edr[1, 0, 8 - strips : 8], total[0 : n - strips]], axis=0)
-    right = jnp.concatenate([total[strips:n], edr[0, 1, 0:strips] + edr[1, 1, 0:strips]], axis=0)
+    left = jnp.concatenate([edr[0, 0] + edr[1, 0], total[0 : n - strips]], axis=0)
+    right = jnp.concatenate([total[strips:n], edr[0, 1] + edr[1, 1]], axis=0)
     sel[0:n] = total[0:n] + 0.5 * (left + right)
 
     @pl.when(passes)
@@ -342,14 +341,11 @@
         copy.wait_send()
 
 
-def finish(gin, inner, sel, c_hbm, green, scat, coup, sout, sem):
+def finish(gin, inner, sel, coup, green, scat, sout, sem):
     count, orbs, lanes = inner.shape[0], inner.shape[2], sel.shape[1]
     strips = orbs // lanes
     stores = [pltpu.make_async_copy(gin, green.at[0], sem.at[count])]
     stores[0].start()
-    fetch = pltpu.make_async_copy(c_hbm, coup, sem.at[count + 1])
-    fetch.start()
-    fetch.wait()
     for k in range(count):
         row = jnp.concatenate([sel[k * strips + i : k * strips + i + 1, :] for i in range(strips)], axis=1)
         rows = pl.ds(k * orbs, orbs)
@@ -368,7 +364,7 @@
     lanes = 128
     vmem = pltpu.VMEM
     dma = pltpu.SemaphoreType.DMA
-    small = 16
+    small = count * orbs // lanes
     hbm = pl.BlockSpec(memory_space=pltpu.HBM)
     in_vmem = pl.BlockSpec(memory_space=pltpu.VMEM)
     struct = jax.ShapeDtypeStruct
@@ -398,8 +394,8 @@
             vmem((ny - 1, small, lanes), F32),
             vmem((3, small, lanes), F32),
             vmem((small, lanes), F32),
-            vmem((2, 2, 8, lanes), F32),
-            vmem((2, 2, 8, lanes), F32),
+            vmem((2, 2, orbs // lanes, lanes), F32),
+            vmem((2, 2, orbs // lanes, lanes), F32),
             dma((count + 4,)),
             dma((PIECES,)),
             dma((PIECES,)),
@@ -425,9 +421,9 @@
     return pl.pallas_call(
         finish,
         out_shape=(out, out),
-        in_specs=[in_vmem, in_vmem, in_vmem, hbm],
+        in_specs=[in_vmem] * 4,
         out_specs=(hbm, hbm),
-        scratch_shapes=[*coupled, vmem((rows, cols), F32), dma((count + 2,))],
+        scratch_shapes=[vmem((rows, cols), F32), dma((count + 1,))],
         compiler_params=pltpu.CompilerParams(vmem_limit_bytes=16 * 2**20),
         name="finish",
     )(green, inner, sel, coupling)

time: 78 us -> 77.5 us (level)
  no operation moved by 1% of the time
where the time goes in v6:
time: 77.5 us; the launch traced here: 77.4 us
  Pallas kernels  76.7 us (99%)
    pallas_call x1, Pallas kernels, body(): pl.pallas_call(functools.partial(kernel, (cuts, energies, groups, count))...  75.3 us

profile of v6, /device:TPU:352, one launch (start us, length us, event | category | flops | bytes accessed | tf_op | source)
XLA Modules:
  0.0 77.4 jit_solution(14731958851584245703)
XLA Ops:
  0.6 0.0 copy-start
  0.6 75.3 %propagate.1 = (f32[1536,128]{1,0:T(8,128)S(1)}, f32[3,128,512]{2,1,0:T(8,128)S(1)}, f32[12,128]{1,0:T(8,128)S(1)}) custom-call(f32[1,3,512,512]{3,2,1,0:T(8,128)} %t_hbm.1, f32[1,1536,128]{2,1,0:T(8,128)} %s_hbm.1, bf16[512,512]{1,0:T(8,128)(2,1)} %coup.1, f32[8]{0:T(128)} %strength_hbm.1, s32[8]{0:T(128)} %shift_hbm.1), custom_call_target="tpu_custom_call" | custom-call | tf_op jit(solution)/shard_map/propagate/pallas_call | solution.py:372
  76.0 0.0 copy-done
  76.0 1.4 %finish.1 = (f32[1,1536,128]{2,1,0:T(8,128)}, f32[1,1536,128]{2,1,0:T(8,128)}) custom-call(f32[1536,128]{1,0:T(8,128)S(1)} %get-tuple-element.5.gin, f32[3,128,512]{2,1,0:T(8,128)S(1)} %get-tuple-element.6.inner, f32[12,128]{1,0:T(8,128)S(1)} %get-tuple-element.7.sel, bf16[512,512]{1,0:T(8,128)(2,1)S(1)} %copy-done), custom_call_target="tpu_custom_call" | custom-call | tf_op jit(solution)/shard_map/finish/pallas_call | solution.py:421
Async XLA Ops:
  0.6 75.3 %copy-start = (bf16[512,512]{1,0:T(8,128)(2,1)S(1)}, bf16[512,512]{1,0:T(8,128)(2,1)}, u32[]{:S(2)}) copy-start(bf16[512,512]{1,0:T(8,128)(2,1)} %coup.1) | copy-start | bytes 1572868
